TPU v7x, 32 devices: a whole 2x2x4 slice. The times are simulated.
32 devices in a mesh: dp: 8 (over z, x), tensor: 4 (over y, core).
Axes of the slice: x: 2, y: 2, z: 4, core: 2. Of those that a mesh axis runs over, the one named last changes fastest.
Arguments:
- layer_input: bfloat16 [12288, 768], P('dp'), may hold values from -6 to 6
- patch_coords: int32 [3, 12288], P(None, 'dp'), may hold values from 0 to 55, as said below
- item_lengths: int32 [32], P('dp'), may hold values from 0 to 1536, as said below
- out_grad: bfloat16 [12288, 768], P('dp'), may hold values from -6 to 6
- ln1_gain: bfloat16 [768], replicated, may hold values from 0.25 to 1.75
- ln1_shift: bfloat16 [768], replicated, may hold values from -1.75 to 1.75
- w_qkv: bfloat16 [768, 3, 768], P(None, None, 'tensor'), may hold values from -0.21875 to 0.21875
- b_qv: bfloat16 [2, 768], P(None, 'tensor'), may hold values from -3 to 3
- w_out: bfloat16 [768, 768], P('tensor'), may hold values from -0.875 to 0.875
- b_out: bfloat16 [768], replicated, may hold values from -1.75 to 1.75
- ln2_gain: bfloat16 [768], replicated, may hold values from 0.25 to 1.75
- ln2_shift: bfloat16 [768], replicated, may hold values from -1.75 to 1.75
- w_fc1: bfloat16 [768, 3072], P(None, 'tensor'), may hold values from -0.21875 to 0.21875
- b_fc1: bfloat16 [3072], P('tensor'), may hold values from -3 to 3
- w_fc2: bfloat16 [3072, 768], P('tensor'), may hold values from -0.109375 to 0.109375
- b_fc2: bfloat16 [768], replicated, may hold values from -1.75 to 1.75
Outputs:
- layer_output: bfloat16 [12288, 768], P('dp')
- input_grad: float32 [12288, 768], P('dp')
- grad_ln1_gain: float32 [768], replicated
- grad_ln1_shift: float32 [768], replicated
- grad_w_qkv: float32 [768, 3, 768], P(None, None, 'tensor')
- grad_b_qv: float32 [2, 768], P(None, 'tensor')
- grad_w_out: float32 [768, 768], P('tensor')
- grad_b_out: float32 [768], replicated
- grad_ln2_gain: float32 [768], replicated
- grad_ln2_shift: float32 [768], replicated
- grad_w_fc1: float32 [768, 3072], P(None, 'tensor')
- grad_b_fc1: float32 [3072], P('tensor')
- grad_w_fc2: float32 [3072, 768], P('tensor')
- grad_b_fc2: float32 [768], replicated
Inputs may be any that keep to these rules, and one draw needn't show every extreme that they name: `item_lengths`: A row of 8 takes 4 consecutive entries: its items' visible lengths, laid out one after another from the row's first slot, summing to at most 1536; the remaining slots are padding. In every draw some row holds a single item of 1536 tokens. `patch_coords`: row 0 is the token's frame, 0 to 2; rows 1 and 2 are its patch row and column.
All inputs are finite; a program needn't handle non-finite values.
Results may differ from a plain program's by a relative error of at most 0.018.
Values may be sent and summed in bfloat16 or wider, within the bound.
A program may use at most 128 MiB of HBM per device.

v0:
```python
from functools import partial
import math

import jax
import jax.numpy as jnp
from jax import lax
from jax.sharding import PartitionSpec as P

HEAD_DIM = 64


NORM_EPS = 1e-06
MASK_FILL = -1e30


def layer_norm(values_in, norm_gain, norm_shift):
    mean_row = jnp.mean(values_in, axis=-1, keepdims=True)
    centred = values_in - mean_row
    spread = jnp.mean(centred * centred, axis=-1, keepdims=True)
    return centred * lax.rsqrt(spread + NORM_EPS) * norm_gain + norm_shift


def sincos_table(coords, feature_count):
    half_width = feature_count // 6
    ladder = jnp.arange(half_width, dtype=jnp.float32) / half_width
    frequency = jnp.power(10000.0, -ladder)
    angles = coords.astype(jnp.float32)[:, :, None] * frequency[None, None, :]
    wave_parts = jnp.concatenate([jnp.sin(angles), jnp.cos(angles)], axis=2)
    return jnp.concatenate([wave_parts[0], wave_parts[1], wave_parts[2]], axis=1)


def item_layout(length_rows, token_count, slot_count):
    item_ends = jnp.cumsum(length_rows, axis=1, dtype=jnp.int32)
    places = jnp.arange(token_count, dtype=jnp.int32)
    passed = (places[None, :, None] >= item_ends[:, None, :]).astype(jnp.int32)
    item_of = jnp.sum(passed, axis=2, dtype=jnp.int32)
    visible = places[None, :] < item_ends[:, -1:]
    return (jnp.where(visible, item_of, slot_count + places[None, :]), visible)


def block_scores(query_block, key_rows, segment_block, segment):
    score_scale = 1.0 / math.sqrt(key_rows.shape[2])
    scores = (
        jnp.einsum("qhd,khd->hqk", query_block, key_rows, preferred_element_type=jnp.float32)
        * score_scale
    )
    allowed = (segment_block[:, None] == segment[None, :])[None]
    return jnp.where(allowed, scores, MASK_FILL)


def attend_forward(query_rows, key_rows, value_rows, segment):
    row_count = query_rows.shape[0]
    block_rows = min(512, row_count)

    def attend_block(block_index):
        block_start = block_index * block_rows
        query_block = lax.dynamic_slice_in_dim(query_rows, block_start, block_rows, 0)
        segment_block = lax.dynamic_slice_in_dim(segment, block_start, block_rows, 0)
        scores = block_scores(query_block, key_rows, segment_block, segment)
        row_max = jnp.max(scores, axis=2, keepdims=True)
        raised = jnp.exp(scores - row_max)
        row_total = jnp.sum(raised, axis=2, keepdims=True)
        weights = (raised / row_total).astype(jnp.bfloat16)
        mixed = jnp.einsum("hqk,khd->qhd", weights, value_rows, preferred_element_type=jnp.float32)
        return (mixed, (row_max + jnp.log(row_total))[:, :, 0])

    mixed_all, log_totals = lax.map(attend_block, jnp.arange(row_count // block_rows))
    return (mixed_all.reshape(query_rows.shape), log_totals)


def attend_backward(query_rows, key_rows, value_rows, segment, mixed_grad, log_totals):
    row_count = query_rows.shape[0]
    block_rows = min(512, row_count)
    score_scale = 1.0 / math.sqrt(key_rows.shape[2])
    zeros_kv = jnp.zeros(key_rows.shape, jnp.float32)

    def back_block(running, inputs):
        block_index, lse_block = inputs
        key_acc, value_acc = running
        block_start = block_index * block_rows
        query_block = lax.dynamic_slice_in_dim(query_rows, block_start, block_rows, 0)
        segment_block = lax.dynamic_slice_in_dim(segment, block_start, block_rows, 0)
        grad_block = lax.dynamic_slice_in_dim(mixed_grad, block_start, block_rows, 0)
        scores = block_scores(query_block, key_rows, segment_block, segment)
        weights = jnp.exp(scores - lse_block[:, :, None])
        weight_grad = jnp.einsum(
            "qhd,khd->hqk", grad_block, value_rows, preferred_element_type=jnp.float32
        )
        centre = jnp.sum(weights * weight_grad, axis=2, keepdims=True)
        score_grad = (weights * (weight_grad - centre)).astype(jnp.bfloat16)
        query_grad = (
            jnp.einsum("hqk,khd->qhd", score_grad, key_rows, preferred_element_type=jnp.float32)
            * score_scale
        )
        key_acc = (
            key_acc
            + jnp.einsum(
                "hqk,qhd->khd", score_grad, query_block, preferred_element_type=jnp.float32
            )
            * score_scale
        )
        value_acc = value_acc + jnp.einsum(
            "hqk,qhd->khd",
            weights.astype(jnp.bfloat16),
            grad_block,
            preferred_element_type=jnp.float32,
        )
        return ((key_acc, value_acc), query_grad)

    block_list = jnp.arange(row_count // block_rows)
    (key_grad, value_grad), query_grad = lax.scan(
        back_block, (zeros_kv, zeros_kv), (block_list, log_totals)
    )
    return (query_grad.reshape(query_rows.shape), key_grad, value_grad)


def run_forward(hidden_in, segment, visible, params, second_pass):
    (
        ln1_gain,
        ln1_shift,
        w_qkv,
        b_qv,
        w_out,
        b_out,
        ln2_gain,
        ln2_shift,
        w_fc1,
        b_fc1,
        w_fc2,
        b_fc2,
    ) = params
    row_count = hidden_in.shape[0]
    heads_here = w_out.shape[0] // HEAD_DIM
    head_shape = (row_count, heads_here, HEAD_DIM)
    normed_one = layer_norm(
        hidden_in, ln1_gain.astype(jnp.float32), ln1_shift.astype(jnp.float32)
    ).astype(jnp.bfloat16)
    projected = jnp.einsum("td,dcj->tcj", normed_one, w_qkv, preferred_element_type=jnp.float32)
    query_rows = (
        (projected[:, 0] + b_qv[0].astype(jnp.float32)).astype(jnp.bfloat16).reshape(head_shape)
    )
    key_rows = projected[:, 1].astype(jnp.bfloat16).reshape(head_shape)
    value_rows = (
        (projected[:, 2] + b_qv[1].astype(jnp.float32)).astype(jnp.bfloat16).reshape(head_shape)
    )
    mixed, log_totals = attend_forward(query_rows, key_rows, value_rows, segment)
    mixed_low = mixed.reshape(row_count, -1).astype(jnp.bfloat16)
    attn_part = jnp.dot(mixed_low, w_out, preferred_element_type=jnp.float32).astype(jnp.bfloat16)
    if second_pass:
        attn_total = lax.psum(attn_part, "tensor").astype(jnp.float32)
    else:
        attn_total = lax.psum(attn_part, "tensor").astype(jnp.float32)
    middle = hidden_in + attn_total + b_out.astype(jnp.float32)
    normed_two = layer_norm(
        middle, ln2_gain.astype(jnp.float32), ln2_shift.astype(jnp.float32)
    ).astype(jnp.bfloat16)
    hidden_pre = jnp.dot(normed_two, w_fc1, preferred_element_type=jnp.float32) + b_fc1.astype(
        jnp.float32
    )
    activated = jax.nn.gelu(hidden_pre, approximate=False).astype(jnp.bfloat16)
    kept_state = (
        normed_one,
        query_rows,
        key_rows,
        value_rows,
        log_totals,
        mixed_low,
        middle,
        normed_two,
        hidden_pre,
        activated,
    )
    if second_pass:
        return (None, kept_state)
    mlp_part = jnp.dot(activated, w_fc2, preferred_element_type=jnp.float32).astype(jnp.bfloat16)
    mlp_total = lax.psum(mlp_part, "tensor").astype(jnp.float32)
    result = jnp.where(visible[:, None], middle + mlp_total + b_fc2.astype(jnp.float32), 0.0)
    return (result, kept_state)


def on_device(
    layer_input,
    patch_coords,
    item_lengths,
    out_grad,
    ln1_gain,
    ln1_shift,
    w_qkv,
    b_qv,
    w_out,
    b_out,
    ln2_gain,
    ln2_shift,
    w_fc1,
    b_fc1,
    w_fc2,
    b_fc2,
):
    segment_rows, visible_rows = item_layout(
        item_lengths.reshape(1, -1), layer_input.shape[0], item_lengths.shape[0]
    )
    segment = segment_rows[0]
    visible = visible_rows[0]
    hidden_in = layer_input.astype(jnp.float32) + sincos_table(patch_coords, layer_input.shape[1])
    params = (
        ln1_gain,
        ln1_shift,
        w_qkv,
        b_qv,
        w_out,
        b_out,
        ln2_gain,
        ln2_shift,
        w_fc1,
        b_fc1,
        w_fc2,
        b_fc2,
    )
    result, kept_state = run_forward(hidden_in, segment, visible, params, False)
    hidden_again = lax.optimization_barrier(hidden_in)
    unused_out, kept_state = run_forward(hidden_again, segment, visible, params, True)
    (
        normed_one,
        query_rows,
        key_rows,
        value_rows,
        log_totals,
        mixed_low,
        middle,
        normed_two,
        hidden_pre,
        activated,
    ) = kept_state
    top_grad = jnp.where(visible[:, None], out_grad, jnp.zeros_like(out_grad))
    top_grad_wide = top_grad.astype(jnp.float32)
    grad_b_fc2 = jnp.sum(top_grad_wide, axis=0)
    grad_w_fc2 = jnp.einsum("tf,td->fd", activated, top_grad, preferred_element_type=jnp.float32)
    act_grad = jnp.einsum("td,fd->tf", top_grad, w_fc2, preferred_element_type=jnp.float32)
    gelu_value, gelu_back = jax.vjp(partial(jax.nn.gelu, approximate=False), hidden_pre)
    pre_grad = gelu_back(act_grad)[0].astype(jnp.bfloat16)
    grad_b_fc1 = jnp.sum(pre_grad.astype(jnp.float32), axis=0)
    grad_w_fc1 = jnp.einsum("td,tf->df", normed_two, pre_grad, preferred_element_type=jnp.float32)
    norm_grad_part = jnp.einsum("tf,df->td", pre_grad, w_fc1, preferred_element_type=jnp.float32)
    norm_grad_two = lax.psum(norm_grad_part.astype(jnp.bfloat16), "tensor").astype(jnp.float32)
    unused_two, norm_back_two = jax.vjp(
        layer_norm, middle, ln2_gain.astype(jnp.float32), ln2_shift.astype(jnp.float32)
    )
    middle_ln, grad_ln2_gain, grad_ln2_shift = norm_back_two(norm_grad_two)
    middle_grad = top_grad_wide + middle_ln
    grad_b_out = jnp.sum(middle_grad, axis=0)
    middle_low = middle_grad.astype(jnp.bfloat16)
    grad_w_out = jnp.einsum("tj,td->jd", mixed_low, middle_low, preferred_element_type=jnp.float32)
    mixed_grad = (
        jnp.einsum("td,jd->tj", middle_low, w_out, preferred_element_type=jnp.float32)
        .astype(jnp.bfloat16)
        .reshape(query_rows.shape)
    )
    query_grad, key_grad, value_grad = attend_backward(
        query_rows, key_rows, value_rows, segment, mixed_grad, log_totals
    )
    row_count = query_rows.shape[0]
    proj_grad = (
        jnp.stack([query_grad, key_grad, value_grad], axis=1)
        .astype(jnp.bfloat16)
        .reshape(row_count, 3, -1)
    )
    grad_b_qv = jnp.sum(proj_grad[:, 0::2].astype(jnp.float32), axis=0)
    grad_w_qkv = jnp.einsum(
        "td,tcj->dcj", normed_one, proj_grad, preferred_element_type=jnp.float32
    )
    norm_grad_first = jnp.einsum(
        "tcj,dcj->td", proj_grad, w_qkv, preferred_element_type=jnp.float32
    )
    norm_grad_one = lax.psum(norm_grad_first.astype(jnp.bfloat16), "tensor").astype(jnp.float32)
    unused_one, norm_back_one = jax.vjp(
        layer_norm, hidden_in, ln1_gain.astype(jnp.float32), ln1_shift.astype(jnp.float32)
    )
    input_ln, grad_ln1_gain, grad_ln1_shift = norm_back_one(norm_grad_one)
    input_grad = middle_grad + input_ln
    (
        grad_ln1_gain,
        grad_ln1_shift,
        grad_w_qkv,
        grad_b_qv,
        grad_w_out,
        grad_b_out,
        grad_ln2_gain,
        grad_ln2_shift,
        grad_w_fc1,
        grad_b_fc1,
        grad_w_fc2,
        grad_b_fc2,
    ) = lax.psum(
        (
            grad_ln1_gain,
            grad_ln1_shift,
            grad_w_qkv,
            grad_b_qv,
            grad_w_out,
            grad_b_out,
            grad_ln2_gain,
            grad_ln2_shift,
            grad_w_fc1,
            grad_b_fc1,
            grad_w_fc2,
            grad_b_fc2,
        ),
        "dp",
    )
    return (
        result.astype(jnp.bfloat16),
        input_grad,
        grad_ln1_gain,
        grad_ln1_shift,
        grad_w_qkv,
        grad_b_qv,
        grad_w_out,
        grad_b_out,
        grad_ln2_gain,
        grad_ln2_shift,
        grad_w_fc1,
        grad_b_fc1,
        grad_w_fc2,
        grad_b_fc2,
    )


def solution(mesh):
    placed = (
        P("dp", None),
        P(None, "dp"),
        P("dp"),
        P("dp", None),
        P(),
        P(),
        P(None, None, "tensor"),
        P(None, "tensor"),
        P("tensor", None),
        P(),
        P(),
        P(),
        P(None, "tensor"),
        P("tensor"),
        P("tensor", None),
        P(),
    )
    return jax.shard_map(
        on_device,
        mesh=mesh,
        in_specs=placed,
        out_specs=(
            P("dp", None),
            P("dp", None),
            P(),
            P(),
            P(None, None, "tensor"),
            P(None, "tensor"),
            P("tensor", None),
            P(),
            P(),
            P(),
            P(None, "tensor"),
            P("tensor"),
            P("tensor", None),
            P(),
        ),
        check_vma=False,
    )
```

profile of v0, /device:TPU:0, one launch (start us, length us, event | category | flops | bytes accessed | tf_op | source)
XLA Modules:
  0.0 919.7 jit_solution(9135779898995659790)
XLA Ops:
  12.9 8.3 multiply_sine_fusion
  22.8 3.2 fusion.126
  26.1 2.6 reduce_sum.227
  28.7 3.1 multiply_reduce_fusion.2
  38.9 38.7 %while.38 = (s32[]{:T(128)}, bf16[3,512,3,64]{1,3,2,0:T(8,128)(2,1)S(1)}, f32[3,3,512]{2,1,0:T(4,128)}, s32[3]{0:T(128)S(1)}, s32[1536]{0:T(1024)}, /*index=5*/s...) while((s32[]{:T(128)}, ...), condition=%wide.region_17.18_spmd, body=%wide.region_14.17_spmd.sunk | while | flops 633076224 | bytes 33306988 | solution.py:67
  44.9 2.8 fusion.197
  47.7 3.6 fusion.198
  57.8 2.8 fusion.197
  60.6 3.6 fusion.198
  70.6 2.8 fusion.197
  73.4 3.6 fusion.198
  78.3 3.4 convolution_convert_fusion.1
  86.9 53.4 %all-reduce.13.cloned.1.call-done = bf16[1536,768]{1,0:T(8,128)(2,1)} async-done(((bf16[1536,768]{1,0:T(8,128)(2,1)}), bf16[1536,768]{1,0:T(8,128)(2,1)}) %all-reduce.13.cloned.1.call-update) | async-done | bytes 2359312 | tf_op jit(solution)/shard_map/psum | solution.py:150
  140.3 3.8 fusion.127
  146.5 28.9 %fusion.53 = (f32[1536,768]{1,0:T(8,128)S(1)}, f32[1536,768]{1,0:T(8,128)S(1)}) fusion(f32[768]{0:T(1024)S(1)} %copy-done.62, bf16[1536,768]{1,0:T(8,128)(2,1)S(1)} %add_convert_fusion.1, bf16[768,768]{1,0:T(8,128)(2,1)S(1)} %copy-done), kind=kOutput, calls=%fused_computation.81 | convolution fusion | flops 1886257152 | bytes 12979200 | tf_op jit(solution)/shard_map/dot_general | solution.py:157
  175.5 4.6 convert_reduce_fusion.3
  181.5 3.5 convolution_convert_fusion
  185.2 55.6 %all-reduce.15.cloned.1.call-done = bf16[1536,768]{1,0:T(8,128)(2,1)} async-done(((bf16[1536,768]{1,0:T(8,128)(2,1)}), bf16[1536,768]{1,0:T(8,128)(2,1)}) %all-reduce.15.cloned.1.call-update) | async-done | bytes 2359312 | tf_op jit(solution)/shard_map/psum | solution.py:244
  240.8 5.3 convert_reduce_fusion.1
  246.2 5.0 fusion.54
  251.3 5.2 fusion.125
  256.5 2.2 copy-done.5
  261.3 102.9 %while.39 = (s32[]{:T(128)}, f32[1536,3,64]{0,2,1:T(8,128)}, f32[1536,3,64]{0,2,1:T(8,128)S(1)}, bf16[3,512,3,64]{1,3,2,0:T(8,128)(2,1)}, s32[3]{0:T(128)S(1)}, ...) while((s32[]{:T(128)}, f32[1536,3,64]{0,2,1:T(8,128)}, ...), condition=%wide.region_26.27_spmd.clone, body=%wide.region_24.26_spmd.clone.sunk | while | flops 1533540864 | bytes 150878800 | solution.py:111
  266.4 2.4 fusion.208
  268.8 7.2 multiply_reduce_fusion.6
  276.1 9.5 %multiply_convert_fusion.4 = bf16[3,512,1536]{2,1,0:T(8,128)(2,1)} fusion(f32[3,512,1536]{2,1,0:T(8,128)} %get-tuple-element.514, f32[3,512,1536]{2,1,0:T(8,128)} %copy-done.1, f32[3,512]{1,0:T(4,128)S(1)} %get-tuple-element.515), kind=kLoop, calls=%fused_computation.32.clone.1 | loop fusion | flops 7077888 | bytes 23599104 | tf_op jit(solution)/shard_map/while/body/eval_jaxpr/convert_element_type | solution.py:90
  285.5 5.0 fusion.210
  300.7 2.4 fusion.208
  303.1 7.2 multiply_reduce_fusion.6
  310.3 9.5 %multiply_convert_fusion.4 = bf16[3,512,1536]{2,1,0:T(8,128)(2,1)} fusion(f32[3,512,1536]{2,1,0:T(8,128)} %get-tuple-element.514, f32[3,512,1536]{2,1,0:T(8,128)} %copy-done.1, f32[3,512]{1,0:T(4,128)S(1)} %get-tuple-element.515), kind=kLoop, calls=%fused_computation.32.clone.1 | loop fusion | flops 7077888 | bytes 23599104 | tf_op jit(solution)/shard_map/while/body/eval_jaxpr/convert_element_type | solution.py:90
  319.8 5.0 fusion.210
  335.0 2.4 fusion.208
  337.4 7.2 multiply_reduce_fusion.6
  344.6 9.5 %multiply_convert_fusion.4 = bf16[3,512,1536]{2,1,0:T(8,128)(2,1)} fusion(f32[3,512,1536]{2,1,0:T(8,128)} %get-tuple-element.514, f32[3,512,1536]{2,1,0:T(8,128)} %copy-done.1, f32[3,512]{1,0:T(4,128)S(1)} %get-tuple-element.515), kind=kLoop, calls=%fused_computation.32.clone.1 | loop fusion | flops 7077888 | bytes 23599104 | tf_op jit(solution)/shard_map/while/body/eval_jaxpr/convert_element_type | solution.py:90
  354.1 5.0 fusion.210
  364.1 2.5 copy.36
  366.6 2.2 stack.11
  371.4 4.7 bitcast_convert_fusion
  376.1 55.8 %all-reduce.17.cloned.1.call-done = bf16[1536,768]{1,0:T(8,128)(2,1)} async-done(((bf16[1536,768]{1,0:T(8,128)(2,1)}), bf16[1536,768]{1,0:T(8,128)(2,1)}) %all-reduce.17.cloned.1.call-update) | async-done | bytes 2359312 | tf_op jit(solution)/shard_map/psum | solution.py:274
  432.0 4.7 fusion.48
  437.3 4.2 fusion.68
  443.3 81.7 %while.37 = (s32[]{:T(128)}, bf16[3,512,3,64]{1,3,2,0:T(8,128)(2,1)S(1)}, s32[3]{0:T(128)S(1)}, s32[1536]{0:T(1024)}, s32[1,1536]{1,0:T(1,128)S(1)}, /*index=5*/...) while((s32[]{:T(128)}, ...), condition=%wide.region_7.8_spmd, body=%wide.region_4.7_spmd.sunk | while | flops 623642112 | bytes 43489504 | solution.py:67
  445.9 5.1 fusion.191
  450.9 14.3 %fusion.192 = (f32[3,512]{1,0:T(4,128)S(1)}, f32[3,512,1536]{2,1,0:T(8,128)}) fusion(f32[3,512,1536]{2,1,0:T(8,128)} %fusion.191, pred[512,1536]{1,0:T(8,128)(4,1)S(1)} %broadcast_compare_fusion.6), kind=kOutput, calls=%fused_computation.226.clone.1 | output fusion | flops 14157311 | bytes 19666944 | tf_op jit(solution)/shard_map/while/body/eval_jaxpr/sub | solution.py:61
  465.2 5.3 fusion.193
  473.1 5.1 fusion.191
  478.1 14.3 %fusion.192 = (f32[3,512]{1,0:T(4,128)S(1)}, f32[3,512,1536]{2,1,0:T(8,128)}) fusion(f32[3,512,1536]{2,1,0:T(8,128)} %fusion.191, pred[512,1536]{1,0:T(8,128)(4,1)S(1)} %broadcast_compare_fusion.6), kind=kOutput, calls=%fused_computation.226.clone.1 | output fusion | flops 14157311 | bytes 19666944 | tf_op jit(solution)/shard_map/while/body/eval_jaxpr/sub | solution.py:61
  492.4 5.3 fusion.193
  500.3 5.1 fusion.191
  505.4 14.3 %fusion.192 = (f32[3,512]{1,0:T(4,128)S(1)}, f32[3,512,1536]{2,1,0:T(8,128)}) fusion(f32[3,512,1536]{2,1,0:T(8,128)} %fusion.191, pred[512,1536]{1,0:T(8,128)(4,1)S(1)} %broadcast_compare_fusion.6), kind=kOutput, calls=%fused_computation.226.clone.1 | output fusion | flops 14157311 | bytes 19666944 | tf_op jit(solution)/shard_map/while/body/eval_jaxpr/sub | solution.py:61
  519.7 5.3 fusion.193
  525.7 2.2 convolution_convert_fusion.3
  528.2 8.1 fusion.69
  536.3 47.6 %all-reduce.9.cloned.1.call-done = bf16[1536,768]{1,0:T(8,128)(2,1)} async-done(((bf16[1536,768]{1,0:T(8,128)(2,1)}), bf16[1536,768]{1,0:T(8,128)(2,1)}) %all-reduce.9.cloned.1.call-update) | async-done | bytes 2359312 | tf_op jit(solution)/shard_map/psum | solution.py:152
  583.9 3.9 fusion.121
  587.9 6.0 fusion.55
  594.5 17.5 %convolution_convert_fusion.2 = bf16[1536,768]{1,0:T(8,128)(2,1)} fusion(bf16[768,768]{1,0:T(8,128)(2,1)} %param.36, bf16[768,768]{1,0:T(8,128)(2,1)S(1)} %copy-done, f32[768]{0:T(1024)} %convert_element_type.190, f32[768]{0:T(1024)} %convert_element_type.188, f32[768]{0:T(1024)} %convert_element_type.187, f32[1536]{0:T(1024)} %add_rsqrt_fusion.1, ...), kind=kOutput, calls=%fused_computation.133 | convolution fusion | flops 3712352256 | bytes 11821056 | tf_op jit(solution)/shard_map/dot_general | solution.py:175
  612.3 6.0 fusion.132
  618.6 4.5 fusion.85
  623.1 2.7 fusion.133
  629.3 38.4 %all-reduce = (f32[768]{0:T(1024)}, f32[768]{0:T(1024)}, f32[2,192]{1,0:T(2,128)}, f32[768]{0:T(1024)}, f32[768]{0:T(1024)}, /*index=5*/f32[768]{0:T(1024)}, f32[768]{0:T(1024)}, f32[768]{0:T(1024)}) all-reduce(f32[768]{0:T(1024)} %get-tuple-element.215, f32[768]{0:T(1024)} %get-tuple-element.222, ...), channel_id=1, replica_groups=mesh['dp'=8,'tensor'=4] {'dp'}, use_global_device_ids=true, to_apply=%region_31.32 | all-reduce | flops 5760 | bytes 46080 | tf_op jit(solution)/shard_map/psum | solution.py:293
  668.9 9.9 %add_add_fusion.2 = (f32[1536,768]{1,0:T(8,128)}, bf16[1536,768]{1,0:T(8,128)(2,1)}) fusion(f32[1536,768]{1,0:T(8,128)} %copy-done.5, f32[1536]{0:T(1024)} %negate_multiply_fusion.2, f32[1536]{0:T(1024)} %get-tuple-element.319, f32[1536,768]{1,0:T(8,128)} %get-tuple-element.298, f32[1536]{0:T(1024)S(1)} %broadcast_multiply_fusion.3, f32[1536]{0:T(1024)} %copy-done.46, ...), kind=kLoop, calls=%fused_computation.88 | loop fusion | flops 20054016 | bytes 23628288 | tf_op jit(solution)/shard_map/add | solution.py:279
  678.8 226.1 %all-reduce.19.cloned.1.call-done = (f32[768,3,192]{0,2,1:T(8,128)}, f32[192,768]{1,0:T(8,128)}, f32[768,768]{1,0:T(8,128)}, f32[768,768]{1,0:T(8,128)}) async-done(((f32[768,3,192]{0,2,1:T(8,128)}, f32[192,768]{1,0:T(8,128)}, f32[768,768]{1,0:T(8,128)}, f32[768,768]{1,0:T(8,128)}), (f32[768,3,192]{0,2,1:T(8,128)}, f32[192,768]{1,0:T(8,128)}, f32[768,768]{1,0:T(8,128)}, ...) | async-done | bytes 7077904 | tf_op jit(solution)/shard_map/psum | solution.py:293
  905.0 2.9 copy.80
  (323 shorter events, 94.2 us)
Async XLA Ops:
  7.2 139.3 %copy-start = (bf16[768,768]{1,0:T(8,128)(2,1)S(1)}, bf16[768,768]{1,0:T(8,128)(2,1)}, u32[]{:S(2)}) copy-start(bf16[768,768]{1,0:T(8,128)(2,1)} %param.34) | copy-start | bytes 3538948
  7.2 133.1 %all-reduce.13.cloned.1.call-start = ((), (), s32[]{:S(2)}) async-start(), calls=%async_computation.2 | async-start | bytes 4718592 | tf_op jit(solution)/shard_map/psum | solution.py:150
  11.4 20.4 %copy-start.38 = (f32[768]{0:T(1024)}, f32[768]{0:T(1024)S(1)}, u32[]{:S(2)}) copy-start(f32[768]{0:T(1024)S(1)} %convert_element_type.176) | copy-start | bytes 9220
  12.1 19.8 %copy-start.59 = (f32[768]{0:T(1024)}, f32[768]{0:T(1024)S(1)}, u32[]{:S(2)}) copy-start(f32[768]{0:T(1024)S(1)} %convert_element_type.177) | copy-start | bytes 9220
  47.7 4.2 copy-start.72
  60.5 4.2 copy-start.72
  73.4 4.2 copy-start.72
  77.6 66.5 %copy-start.8 = (bf16[1536,3,64]{0,2,1:T(8,128)(2,1)}, bf16[1536,3,64]{0,2,1:T(8,128)(2,1)S(1)}, u32[]{:S(2)}) copy-start(bf16[1536,3,64]{0,2,1:T(8,128)(2,1)S(1)} %get-tuple-element.668) | copy-start | bytes 1769476
  77.6 4.2 copy-start.65
  78.3 65.8 %copy-start.13 = (bf16[24,8,3,512]{3,1,2,0:T(8,128)(2,1)}, bf16[24,8,3,512]{3,1,2,0:T(8,128)(2,1)S(1)}, u32[]{:S(2)}) copy-start(bf16[24,8,3,512]{3,1,2,0:T(8,128)(2,1)S(1)} %copy.38) | copy-start | bytes 1769476
  81.7 159.1 %all-reduce.15.cloned.1.call-start = ((), (), s32[]{:S(2)}) async-start(), calls=%async_computation.3 | async-start | bytes 4718592 | tf_op jit(solution)/shard_map/psum | solution.py:244
  81.8 62.3 %copy-start.41 = (f32[768]{0:T(1024)}, f32[768]{0:T(1024)S(1)}, u32[]{:S(2)}) copy-start(f32[768]{0:T(1024)S(1)} %convert_element_type.186) | copy-start | bytes 9220
  144.8 30.5 %copy-start.48 = (f32[1536]{0:T(1024)}, f32[1536]{0:T(1024)S(1)}, u32[]{:S(2)}) copy-start(f32[1536]{0:T(1024)S(1)} %multiply_reduce_fusion.1) | copy-start | bytes 18436
  144.9 30.5 %copy-start.36 = (f32[1536]{0:T(1024)}, f32[1536]{0:T(1024)S(1)}, u32[]{:S(2)}) copy-start(f32[1536]{0:T(1024)S(1)} %fusion.89) | copy-start | bytes 18436
  146.4 29.0 %copy-start.12 = (bf16[1536,768]{1,0:T(8,128)(2,1)}, bf16[1536,768]{1,0:T(8,128)(2,1)S(1)}, u32[]{:S(2)}) copy-start(bf16[1536,768]{1,0:T(8,128)(2,1)S(1)} %add_convert_fusion.1) | copy-start | bytes 7077892
  146.5 29.0 %copy-start.30 = (bf16[1536,768]{1,0:T(8,128)(2,1)S(1)}, bf16[1536,768]{1,0:T(8,128)(2,1)}, u32[]{:S(2)}) copy-start(bf16[1536,768]{1,0:T(8,128)(2,1)} %param.25) | copy-start | bytes 7077892
  146.5 29.0 %copy-start.56 = (pred[1536]{0:T(1024)(128)(4,1)S(1)}, pred[1536]{0:T(1024)(128)(4,1)}, u32[]{:S(2)}) copy-start(pred[1536]{0:T(1024)(128)(4,1)} %iota_compare_fusion.1) | copy-start | bytes 4612
  146.5 29.0 %copy-start.66 = (bf16[768,768]{1,0:T(8,128)(2,1)S(1)}, bf16[768,768]{1,0:T(8,128)(2,1)}, u32[]{:S(2)}) copy-start(bf16[768,768]{1,0:T(8,128)(2,1)} %param.36) | copy-start | bytes 3538948
  175.4 4.7 copy-start.73
  175.4 4.7 copy-start.74
  184.9 247.0 %all-reduce.17.cloned.1.call-start = ((), (), s32[]{:S(2)}) async-start(), calls=%async_computation.4 | async-start | bytes 4718592 | tf_op jit(solution)/shard_map/psum | solution.py:274
  240.8 5.4 copy-start.49
  240.8 5.4 copy-start.11
  240.8 5.4 copy-start.37
  240.8 5.4 copy-start.44
  246.2 5.1 copy-start.31
  246.2 5.1 copy-start.57
  251.3 7.4 copy-start.16
  268.8 7.2 copy-start.1
  285.5 5.1 copy-start.2
  285.5 5.3 copy-start.28
  303.1 7.2 copy-start.1
  319.8 5.1 copy-start.2
  319.8 5.3 copy-start.28
  337.4 7.2 copy-start.1
  354.1 5.1 copy-start.2
  354.1 5.3 copy-start.28
  368.8 7.3 copy-start.26
  371.4 4.8 copy-start.50
  371.4 60.6 %copy-start.39 = (f32[768]{0:T(1024)S(1)}, f32[768]{0:T(1024)}, u32[]{:S(2)}) copy-start(f32[768]{0:T(1024)} %copy-done.38) | copy-start | bytes 9220
  376.0 61.2 %copy-start.60 = (f32[768]{0:T(1024)S(1)}, f32[768]{0:T(1024)}, u32[]{:S(2)}) copy-start(f32[768]{0:T(1024)} %copy-done.59) | copy-start | bytes 9220
  376.0 61.3 %copy-start.68 = (bf16[768,3,192]{0,2,1:T(8,128)(2,1)S(1)}, bf16[768,3,192]{0,2,1:T(8,128)(2,1)}, u32[]{:S(2)}) copy-start(bf16[768,3,192]{0,2,1:T(8,128)(2,1)} %param.28) | copy-start | bytes 2654212
  376.1 207.8 %all-reduce.9.cloned.1.call-start = ((), (), s32[]{:S(2)}) async-start(), calls=%async_computation | async-start | bytes 4718592 | tf_op jit(solution)/shard_map/psum | solution.py:152
  437.3 4.2 copy-start.46
  443.3 82.4 %copy-start.17 = (bf16[192,768]{1,0:T(8,128)(2,1)S(1)}, bf16[192,768]{1,0:T(8,128)(2,1)}, u32[]{:S(2)}) copy-start(bf16[192,768]{1,0:T(8,128)(2,1)} %param.30) | copy-start | bytes 884740
  450.9 14.3 %copy-start.35 = (bf16[1536,3,64]{0,2,1:T(8,128)(2,1)S(1)}, bf16[1536,3,64]{0,2,1:T(8,128)(2,1)}, u32[]{:S(2)}) copy-start(bf16[1536,3,64]{0,2,1:T(8,128)(2,1)} %get-tuple-element.634) | copy-start | bytes 1769476 | tf_op jit(solution)/shard_map/while
  478.1 14.3 %copy-start.35 = (bf16[1536,3,64]{0,2,1:T(8,128)(2,1)S(1)}, bf16[1536,3,64]{0,2,1:T(8,128)(2,1)}, u32[]{:S(2)}) copy-start(bf16[1536,3,64]{0,2,1:T(8,128)(2,1)} %get-tuple-element.634) | copy-start | bytes 1769476 | tf_op jit(solution)/shard_map/while
  505.4 14.3 %copy-start.35 = (bf16[1536,3,64]{0,2,1:T(8,128)(2,1)S(1)}, bf16[1536,3,64]{0,2,1:T(8,128)(2,1)}, u32[]{:S(2)}) copy-start(bf16[1536,3,64]{0,2,1:T(8,128)(2,1)} %get-tuple-element.634) | copy-start | bytes 1769476 | tf_op jit(solution)/shard_map/while
  528.0 55.9 %copy-start.42 = (f32[768]{0:T(1024)S(1)}, f32[768]{0:T(1024)}, u32[]{:S(2)}) copy-start(f32[768]{0:T(1024)} %copy-done.41) | copy-start | bytes 9220
  528.0 141.0 %all-reduce.11.cloned.1.call-start = ((), (), s32[]{:S(2)}) async-start(), calls=%async_computation.1 | async-start | bytes 4718592 | tf_op jit(solution)/shard_map/psum | solution.py:176
  536.3 51.5 %copy-start.9 = (bf16[1536,768]{1,0:T(8,128)(2,1)S(1)}, bf16[1536,768]{1,0:T(8,128)(2,1)}, u32[]{:S(2)}) copy-start(bf16[1536,768]{1,0:T(8,128)(2,1)} %all-reduce.17.cloned.1.call-done) | copy-start | bytes 7077892
  536.3 51.5 %copy-start.40 = (f32[768]{0:T(1024)S(1)}, f32[768]{0:T(1024)}, u32[]{:S(2)}) copy-start(f32[768]{0:T(1024)} %copy-done.38) | copy-start | bytes 9220
  583.9 4.0 copy-start.45
  583.9 4.0 copy-start.47
  587.8 6.0 copy-start.51
  612.0 293.0 %all-reduce.19.cloned.1.call-start = ((), (), s32[]{:S(2)}) async-start(), calls=%async_computation.5 | async-start | bytes 14155776 | tf_op jit(solution)/shard_map/psum | solution.py:293
  612.2 6.1 copy-start.21
  612.3 6.1 copy-start.23
  612.3 6.1 copy-start.27
  612.3 6.3 copy-start.14
  618.3 4.8 copy-start.33
  618.6 7.3 copy-start.15
  905.0 4.9 copy-start.25
  905.0 6.3 copy-start.24
  (41 other events, 80.3 us)
Sparse Core Ops, SparseCore 0:
  81.9 58.3 all-reduce.12
  185.1 55.7 all-reduce.14
  376.2 55.7 all-reduce.16
  528.1 55.7 all-reduce.8
  612.1 55.7 all-reduce.10
  673.3 231.6 all-reduce.18
where the time goes:
time: 928 us; the launch traced here: 920 us
  waiting for transfers between devices  439 us (47%)
  matrix products  196 us (21%)
  other arithmetic  176 us (19%)
  local copies, waits for them, and re-layouts  47.8 us (5%)
  blocking collectives  38.4 us (4%)
  between operations  15.2 us (2%)
    psum x1, waiting for transfers between devices, on_device(): lax.psum((grad_ln1_gain, grad_ln1_shift, grad_w_qkv, grad_b_qv, grad_w_ou...  226 us
    psum x2, waiting for transfers between devices, run_forward(): attn_total = lax.psum(attn_part, 'tensor').astype(jnp.float32)  101 us
    psum x1, waiting for transfers between devices, on_device(): lax.psum(norm_grad_first.astype(jnp.bfloat16), 'tensor').astype(jnp.float32)  55.8 us
    psum x1, waiting for transfers between devices, on_device(): lax.psum(norm_grad_part.astype(jnp.bfloat16), 'tensor').astype(jnp.float32)  55.6 us
    dot_general x9, matrix products, block_scores(): jnp.einsum('qhd,khd->hqk', query_block, key_rows, preferred_element_type=...  42.9 us
    sub x3, other arithmetic, attend_block(): raised = jnp.exp(scores - row_max)  42.9 us
    psum x1, blocking collectives, on_device(): lax.psum((grad_ln1_gain, grad_ln1_shift, grad_w_qkv, grad_b_qv, grad_w_ou...  38.4 us
    dot_general x1, matrix products, run_forward(): jnp.dot(normed_two, w_fc1, preferred_element_type=jnp.float32)  28.9 us
  transfers between devices with their start and end apart: 6, of which 5 were waited for; matrix products, arithmetic and copies ran while one was open for 4% of the time, Pallas kernels for 0%

commit v1 on v0

--- a/solution.py
+++ b/solution.py
@@ -178,6 +178,13 @@
     return (result, kept_state)
 
 
+def sum_gradients(grads):
+    large = [g.ndim == 2 and g.shape[0] > 2 or g.ndim == 3 for g in grads]
+    low = lax.psum([g.astype(jnp.bfloat16) for g, w in zip(grads, large) if w], "dp")
+    wide = lax.psum([g for g, w in zip(grads, large) if not w], "dp")
+    return [low.pop(0).astype(jnp.float32) if w else wide.pop(0) for w in large]
+
+
 def on_device(
     layer_input,
     patch_coords,
@@ -217,8 +224,6 @@
         b_fc2,
     )
     result, kept_state = run_forward(hidden_in, segment, visible, params, False)
-    hidden_again = lax.optimization_barrier(hidden_in)
-    unused_out, kept_state = run_forward(hidden_again, segment, visible, params, True)
     (
         normed_one,
         query_rows,
@@ -290,7 +295,7 @@
         grad_b_fc1,
         grad_w_fc2,
         grad_b_fc2,
-    ) = lax.psum(
+    ) = sum_gradients(
         (
             grad_ln1_gain,
             grad_ln1_shift,
@@ -304,8 +309,7 @@
             grad_b_fc1,
             grad_w_fc2,
             grad_b_fc2,
-        ),
-        "dp",
+        )
     )
     return (
         result.astype(jnp.bfloat16),

time: 928 us -> 620 us (0.67)
  waiting for transfers between devices: 439 us -> 269 us
  other arithmetic: 176 us -> 116 us
  matrix products: 196 us -> 139 us
  local copies, waits for them, and re-layouts: 47.8 us -> 29.2 us
    psum x2 -> x1, waiting for transfers between devices: 282 us -> 84.1 us  [sum_gradients(): lax.psum([g.astype(jnp.bfloat16) for g, w in zip(grads, large) if w], 'dp')]
    psum x1, waiting for transfers between devices: 0.01 us -> 80.8 us  [run_forward(): mlp_total = lax.psum(mlp_part, 'tensor').astype(jnp.float32)]
    psum x2 -> x1, waiting for transfers between devices: 101 us -> 53.4 us  [run_forward(): attn_total = lax.psum(attn_part, 'tensor').astype(jnp.float32)]
    sub x3 -> x0, other arithmetic: 42.9 us -> none  [attend_block(): raised = jnp.exp(scores - row_max)]
    dot_general x1, matrix products: 28.9 us -> 12.8 us  [run_forward(): jnp.dot(normed_two, w_fc1, preferred_element_type=jnp.float32)]
    dot_general x6 -> x3, matrix products: 26.7 us -> 10.7 us  [attend_block(): jnp.einsum('hqk,khd->qhd', weights, value_rows, preferred_element_type=jn...]
    convert_element_type x1 -> x6, other arithmetic: 0.13 us -> 13.8 us  [the longest x4 8.05 us: sum_gradients(): return [low.pop(0).astype(jnp.float32) if w else wide.pop(0) for w in large]]
    dot_general x9 -> x6, matrix products: 42.9 us -> 30.4 us  [block_scores(): jnp.einsum('qhd,khd->hqk', query_block, key_rows, preferred_element_type=...]
  transfers between devices with their start and end apart: 6 -> 4, of which waited for: 5 -> 4; matrix products, arithmetic and copies ran while one was open for 4% -> 7% of each run, Pallas kernels for 0% -> 0%
where the time goes in v1:
time: 620 us; the launch traced here: 613 us
  waiting for transfers between devices  269 us (43%)
  matrix products  139 us (22%)
  other arithmetic  116 us (19%)
  blocking collectives  40.6 us (7%)
  local copies, waits for them, and re-layouts  29.2 us (5%)
  between operations  14.8 us (2%)
    psum x1, waiting for transfers between devices, sum_gradients(): lax.psum([g.astype(jnp.bfloat16) for g, w in zip(grads, large) if w], 'dp')  84.1 us
    psum x1, waiting for transfers between devices, run_forward(): mlp_total = lax.psum(mlp_part, 'tensor').astype(jnp.float32)  80.8 us
    psum x1, waiting for transfers between devices, run_forward(): attn_total = lax.psum(attn_part, 'tensor').astype(jnp.float32)  53.4 us
    psum x1, waiting for transfers between devices, on_device(): lax.psum(norm_grad_part.astype(jnp.bfloat16), 'tensor').astype(jnp.float32)  50.4 us
    psum x1, blocking collectives, sum_gradients(): wide = lax.psum([g for g, w in zip(grads, large) if not w], 'dp')  40.6 us
    dot_general x6, matrix products, block_scores(): jnp.einsum('qhd,khd->hqk', query_block, key_rows, preferred_element_type=...  30.4 us
    convert_element_type x3, other arithmetic, back_block(): score_grad = (weights * (weight_grad - centre)).astype(jnp.bfloat16)  28.3 us
    reduce_sum x4, other arithmetic, layer_norm(): return centred * lax.rsqrt(spread + NORM_EPS) * norm_gain + norm_shift  19.9 us
  transfers between devices with their start and end apart: 4, of which 4 were waited for; matrix products, arithmetic and copies ran while one was open for 7% of the time, Pallas kernels for 0%

profile of v1, /device:TPU:0, one launch (start us, length us, event | category | flops | bytes accessed | tf_op | source)
XLA Modules:
  0.0 612.6 jit_solution(17201050054439104026)
XLA Ops:
  8.1 8.3 %multiply_sine_fusion = (f32[3,1536,128]{2,1,0:T(8,128)S(1)}, f32[3,1536,128]{2,1,0:T(8,128)S(1)}) fusion(f32[128]{0:T(128)S(1)} %negate_power_fusion, f32[3,1536]{1,0:T(4,128)S(1)} %convert_element_type.153), kind=kLoop, calls=%fused_computation.89 | loop fusion | flops 589824 | bytes 4737536 | tf_op jit(solution)/shard_map/sin | solution.py:28
  21.2 1.6 fusion.62
  22.8 1.6 fusion.61
  27.4 1.8 add_convert_fusion.3
  29.3 38.7 %while.27 = (s32[]{:T(128)}, bf16[3,512,3,64]{1,3,2,0:T(8,128)(2,1)S(1)}, f32[3,3,512]{2,1,0:T(4,128)}, s32[3]{0:T(128)S(1)}, s32[1536]{0:T(1024)}, /*index=5*/s...) while((s32[]{:T(128)}, ...), condition=%wide.region_7.8_spmd, body=%wide.region_4.7_spmd.sunk | while | flops 633076224 | bytes 33307488 | solution.py:67
  33.3 2.0 fusion.110
  35.3 2.8 fusion.111
  38.8 3.6 fusion.112
  46.2 2.0 fusion.110
  48.2 2.8 fusion.111
  51.6 3.6 fusion.112
  59.0 2.0 fusion.110
  61.0 2.8 fusion.111
  64.4 3.6 fusion.112
  68.7 3.4 convolution_convert_fusion.2
  77.3 53.4 %all-reduce.8.cloned.1.call-done = bf16[1536,768]{1,0:T(8,128)(2,1)} async-done(((bf16[1536,768]{1,0:T(8,128)(2,1)}), bf16[1536,768]{1,0:T(8,128)(2,1)}) %all-reduce.8.cloned.1.call-update) | async-done | bytes 2359312 | tf_op jit(solution)/shard_map/psum | solution.py:152
  130.7 3.8 fusion.59
  135.3 1.3 add_convert_fusion.1
  136.8 12.8 %multiply_convert_fusion.1 = (bf16[1536,768]{1,0:T(8,128)(2,1)}, f32[1536,768]{1,0:T(8,128)S(1)}, f32[1536,768]{1,0:T(8,128)S(1)}) fusion(f32[768]{0:T(1024)S(1)} %copy-done.49, bf16[1536,768]{1,0:T(8,128)(2,1)S(1)} %add_convert_fusion.1, bf16[768,768]{1,0:T(8,128)(2,1)S(1)} %copy-done), kind=kOutput, calls=%fused_computation.69 | convolution fusion | flops 1889796096 | bytes 15338496 | tf_op jit(solution)/shard_map/dot_general | solution.py:157
  149.6 4.6 convert_reduce_fusion.3
  154.2 1.4 copy-done.62
  155.6 3.5 convolution_convert_fusion
  159.1 5.4 convolution_convert_fusion.1
  164.5 50.4 %all-reduce.10.cloned.1.call-done = bf16[1536,768]{1,0:T(8,128)(2,1)} async-done(((bf16[1536,768]{1,0:T(8,128)(2,1)}), bf16[1536,768]{1,0:T(8,128)(2,1)}) %all-reduce.10.cloned.1.call-update) | async-done | bytes 2359312 | tf_op jit(solution)/shard_map/psum | solution.py:249
  214.9 5.3 convert_reduce_fusion.1
  220.3 5.5 fusion.38
  225.9 5.2 fusion.57
  231.1 2.2 copy-done.5
  233.3 1.8 convolution_convert_fusion.3
  236.0 114.1 %while.28 = (s32[]{:T(128)}, f32[1536,3,64]{0,2,1:T(8,128)}, f32[1536,3,64]{0,2,1:T(8,128)S(1)}, bf16[3,512,3,64]{1,3,2,0:T(8,128)(2,1)}, s32[3]{0:T(128)S(1)}, ...) while((s32[]{:T(128)}, f32[1536,3,64]{0,2,1:T(8,128)}, ...), condition=%wide.region_17.18_spmd.clone, body=%wide.region_15.17_spmd.clone.sunk | while | flops 1533540864 | bytes 113105432 | solution.py:111
  237.1 6.0 fusion.122
  245.1 8.1 %multiply_reduce_fusion.4 = (f32[3,512]{1,0:T(4,128)S(1)}, f32[3,512,1536]{2,1,0:T(8,128)}) fusion(f32[3,512,1536]{2,1,0:T(8,128)} %fusion.122, f32[3,512]{1,0:T(4,128)S(1)} %dynamic-slice_bitcast_fusion.2, bf16[1536,3,64]{0,2,1:T(8,128)(2,1)S(1)} %get-tuple-element.476, bf16[1536,3,64]{0,2,1:T(8,128)(2,1)} %get-tuple-element.473, ...), kind=kOutput, calls=%fused_computation.16.clone.1 | convolution fusion | flops 313784832 | bytes 20459524 | tf_op jit(solution)/shard_map/while/body/eval_jaxpr/qhd,khd->hqk/dot_general | solution.py:44
  253.3 9.4 %multiply_convert_fusion.3 = bf16[3,512,1536]{2,1,0:T(8,128)(2,1)} fusion(f32[3,512,1536]{2,1,0:T(8,128)} %get-tuple-element.395, f32[3,512,1536]{2,1,0:T(8,128)} %fusion.122, f32[3,512]{1,0:T(4,128)S(1)} %get-tuple-element.396), kind=kLoop, calls=%fused_computation.15.clone.1 | loop fusion | flops 7077888 | bytes 23599104 | tf_op jit(solution)/shard_map/while/body/eval_jaxpr/convert_element_type | solution.py:90
  262.7 3.6 fusion.123
  266.7 1.5 fusion.125
  269.1 4.9 fusion.124
  275.2 6.0 fusion.122
  283.2 8.1 %multiply_reduce_fusion.4 = (f32[3,512]{1,0:T(4,128)S(1)}, f32[3,512,1536]{2,1,0:T(8,128)}) fusion(f32[3,512,1536]{2,1,0:T(8,128)} %fusion.122, f32[3,512]{1,0:T(4,128)S(1)} %dynamic-slice_bitcast_fusion.2, bf16[1536,3,64]{0,2,1:T(8,128)(2,1)S(1)} %get-tuple-element.476, bf16[1536,3,64]{0,2,1:T(8,128)(2,1)} %get-tuple-element.473, ...), kind=kOutput, calls=%fused_computation.16.clone.1 | convolution fusion | flops 313784832 | bytes 20459524 | tf_op jit(solution)/shard_map/while/body/eval_jaxpr/qhd,khd->hqk/dot_general | solution.py:44
  291.3 9.4 %multiply_convert_fusion.3 = bf16[3,512,1536]{2,1,0:T(8,128)(2,1)} fusion(f32[3,512,1536]{2,1,0:T(8,128)} %get-tuple-element.395, f32[3,512,1536]{2,1,0:T(8,128)} %fusion.122, f32[3,512]{1,0:T(4,128)S(1)} %get-tuple-element.396), kind=kLoop, calls=%fused_computation.15.clone.1 | loop fusion | flops 7077888 | bytes 23599104 | tf_op jit(solution)/shard_map/while/body/eval_jaxpr/convert_element_type | solution.py:90
  300.8 3.6 fusion.123
  304.8 1.5 fusion.125
  307.2 4.9 fusion.124
  313.2 6.0 fusion.122
  321.3 8.1 %multiply_reduce_fusion.4 = (f32[3,512]{1,0:T(4,128)S(1)}, f32[3,512,1536]{2,1,0:T(8,128)}) fusion(f32[3,512,1536]{2,1,0:T(8,128)} %fusion.122, f32[3,512]{1,0:T(4,128)S(1)} %dynamic-slice_bitcast_fusion.2, bf16[1536,3,64]{0,2,1:T(8,128)(2,1)S(1)} %get-tuple-element.476, bf16[1536,3,64]{0,2,1:T(8,128)(2,1)} %get-tuple-element.473, ...), kind=kOutput, calls=%fused_computation.16.clone.1 | convolution fusion | flops 313784832 | bytes 20459524 | tf_op jit(solution)/shard_map/while/body/eval_jaxpr/qhd,khd->hqk/dot_general | solution.py:44
  329.4 9.4 %multiply_convert_fusion.3 = bf16[3,512,1536]{2,1,0:T(8,128)(2,1)} fusion(f32[3,512,1536]{2,1,0:T(8,128)} %get-tuple-element.395, f32[3,512,1536]{2,1,0:T(8,128)} %fusion.122, f32[3,512]{1,0:T(4,128)S(1)} %get-tuple-element.396), kind=kLoop, calls=%fused_computation.15.clone.1 | loop fusion | flops 7077888 | bytes 23599104 | tf_op jit(solution)/shard_map/while/body/eval_jaxpr/convert_element_type | solution.py:90
  338.9 3.6 fusion.123
  342.8 1.5 fusion.125
  345.2 4.9 fusion.124
  350.1 1.6 copy.34
  354.1 4.6 bitcast_convert_fusion
  358.9 5.6 convolution_convert_fusion.5
  364.5 3.3 convolution_convert_fusion.4
  368.0 1.5 fusion.63
  370.6 1.4 convolution_convert_fusion.6
  372.3 80.8 %all-reduce.14.cloned.1.call-done = (bf16[1536,768]{1,0:T(8,128)(2,1)}, bf16[1536,768]{1,0:T(8,128)(2,1)}) async-done(((bf16[1536,768]{1,0:T(8,128)(2,1)}, bf16[1536,768]{1,0:T(8,128)(2,1)}), (bf16[1536,768]{1,0:T(8,128)(2,1)}, bf16[1536,768]{1,0:T(8,128)(2,1)})) %all-reduce.14.cloned.1.call-update) | async-done | bytes 4718608 | tf_op jit(solution)/shard_map/psum | solution.py:176
  453.1 4.7 convert_reduce_fusion
  457.9 4.3 fusion.39
  462.3 40.6 %all-reduce = (f32[768]{0:T(1024)}, f32[768]{0:T(1024)}, f32[2,192]{1,0:T(2,128)}, f32[768]{0:T(1024)}, f32[768]{0:T(1024)}, /*index=5*/f32[768]{0:T(1024)}, f32[768]{0:T(1024)}, f32[768]{0:T(1024)}) all-reduce(f32[768]{0:T(1024)S(1)} %get-tuple-element.172, ...), channel_id=1, replica_groups=mesh['dp'=8,'tensor'=4] {'dp'}, use_global_device_ids=true, to_apply=%region_22.23 | all-reduce | flops 5760 | bytes 46080 | tf_op jit(solution)/shard_map/psum | solution.py:184
  502.9 4.8 select_convert_fusion
  508.9 4.8 add_add_fusion.2
  513.7 84.1 %all-reduce.12.cloned.1.call-done = (bf16[768,3,192]{0,2,1:T(8,128)(2,1)}, bf16[192,768]{1,0:T(8,128)(2,1)}, bf16[768,768]{1,0:T(8,128)(2,1)}, bf16[768,768]{1,0:T(8,128)(2,1)}) async-done(((bf16[768,3,192]{0,2,1:T(8,128)(2,1)}, bf16[192,768]{1,0:T(8,128)(2,1)}, bf16[768,768]{1,0:T(8,128)(2,1)}, bf16[768,768]{1,0:T(8,128)(2,1)}), (bf16[768,3,192]{0,2,1:T(8,128)(2,1)}, bf16[192,768]{1,0:T(8,128)(2,1)}, ...) | async-done | bytes 3538960 | tf_op jit(solution)/shard_map/psum | solution.py:183
  597.8 3.0 convert_element_type.189
  600.8 2.8 convert_element_type.192
  603.6 1.4 convert_element_type.184
  (258 shorter events, 44.9 us)
Async XLA Ops:
  7.2 129.5 %copy-start = (bf16[768,768]{1,0:T(8,128)(2,1)S(1)}, bf16[768,768]{1,0:T(8,128)(2,1)}, u32[]{:S(2)}) copy-start(bf16[768,768]{1,0:T(8,128)(2,1)} %param.32) | copy-start | bytes 3538948
  7.2 123.5 %all-reduce.8.cloned.1.call-start = ((), (), s32[]{:S(2)}) async-start(), calls=%async_computation | async-start | bytes 4718592 | tf_op jit(solution)/shard_map/psum | solution.py:152
  20.8 3.6 copy-start.20
  22.8 4.4 copy-start.50
  38.8 3.6 copy-start.61
  51.6 3.6 copy-start.61
  64.4 3.6 copy-start.61
  68.0 66.5 %copy-start.8 = (bf16[1536,3,64]{0,2,1:T(8,128)(2,1)}, bf16[1536,3,64]{0,2,1:T(8,128)(2,1)S(1)}, u32[]{:S(2)}) copy-start(bf16[1536,3,64]{0,2,1:T(8,128)(2,1)S(1)} %get-tuple-element.500) | copy-start | bytes 1769476
  68.0 4.2 copy-start.53
  68.7 65.8 %copy-start.12 = (bf16[24,8,3,512]{3,1,2,0:T(8,128)(2,1)}, bf16[24,8,3,512]{3,1,2,0:T(8,128)(2,1)S(1)}, u32[]{:S(2)}) copy-start(bf16[24,8,3,512]{3,1,2,0:T(8,128)(2,1)S(1)} %copy.35) | copy-start | bytes 1769476
  72.2 142.8 %all-reduce.10.cloned.1.call-start = ((), (), s32[]{:S(2)}) async-start(), calls=%async_computation.1 | async-start | bytes 4718592 | tf_op jit(solution)/shard_map/psum | solution.py:249
  135.2 14.3 %copy-start.38 = (f32[1536]{0:T(1024)}, f32[1536]{0:T(1024)S(1)}, u32[]{:S(2)}) copy-start(f32[1536]{0:T(1024)S(1)} %multiply_reduce_fusion.1) | copy-start | bytes 18436
  135.3 14.3 %copy-start.30 = (f32[1536]{0:T(1024)}, f32[1536]{0:T(1024)S(1)}, u32[]{:S(2)}) copy-start(f32[1536]{0:T(1024)S(1)} %fusion.53) | copy-start | bytes 18436
  136.7 12.8 %copy-start.22 = (bf16[1536,768]{1,0:T(8,128)(2,1)}, bf16[1536,768]{1,0:T(8,128)(2,1)S(1)}, u32[]{:S(2)}) copy-start(bf16[1536,768]{1,0:T(8,128)(2,1)S(1)} %add_convert_fusion.1) | copy-start | bytes 7077892
  136.7 12.8 %copy-start.17 = (bf16[1536,768]{1,0:T(8,128)(2,1)S(1)}, bf16[1536,768]{1,0:T(8,128)(2,1)}, u32[]{:S(2)}) copy-start(bf16[1536,768]{1,0:T(8,128)(2,1)} %param.23) | copy-start | bytes 7077892
  136.7 12.8 %copy-start.40 = (pred[1536]{0:T(1024)(128)(4,1)S(1)}, pred[1536]{0:T(1024)(128)(4,1)}, u32[]{:S(2)}) copy-start(pred[1536]{0:T(1024)(128)(4,1)} %iota_compare_fusion.1) | copy-start | bytes 4612
  136.7 12.8 %copy-start.55 = (bf16[768,768]{1,0:T(8,128)(2,1)S(1)}, bf16[768,768]{1,0:T(8,128)(2,1)}, u32[]{:S(2)}) copy-start(bf16[768,768]{1,0:T(8,128)(2,1)} %param.34) | copy-start | bytes 3538948
  159.0 294.0 %all-reduce.14.cloned.1.call-start = ((), (), s32[]{:S(2)}) async-start(), calls=%async_computation.3 | async-start | bytes 9437184 | tf_op jit(solution)/shard_map/psum | solution.py:176
  159.1 55.8 %copy-start.35 = (f32[768]{0:T(1024)S(1)}, f32[768]{0:T(1024)}, u32[]{:S(2)}) copy-start(f32[768]{0:T(1024)} %convert_element_type.166) | copy-start | bytes 9220
  164.5 55.8 %copy-start.39 = (f32[1536]{0:T(1024)S(1)}, f32[1536]{0:T(1024)}, u32[]{:S(2)}) copy-start(f32[1536]{0:T(1024)} %copy-done.38) | copy-start | bytes 18436
  164.5 55.8 %copy-start.31 = (f32[1536]{0:T(1024)S(1)}, f32[1536]{0:T(1024)}, u32[]{:S(2)}) copy-start(f32[1536]{0:T(1024)} %copy-done.30) | copy-start | bytes 18436
  214.9 5.4 copy-start.11
  220.3 5.6 copy-start.18
  220.3 5.6 copy-start.41
  225.9 7.5 %copy-start.23 = (bf16[192,768]{1,0:T(8,128)(2,1)S(1)}, bf16[192,768]{1,0:T(8,128)(2,1)}, u32[]{:S(2)}) copy-start(bf16[192,768]{1,0:T(8,128)(2,1)} %param.28) | copy-start | bytes 884740
  236.0 7.2 %copy-start.58 = (s32[3]{0:T(128)}, s32[3]{0:T(128)S(1)}, u32[]{:S(2)}) copy-start(s32[3]{0:T(128)S(1)} %get-tuple-element.472) | copy-start | bytes 40 | tf_op jit(solution)/shard_map/while
  253.3 9.5 %copy-start.6 = (f32[1536,3,64]{0,2,1:T(8,128)S(1)}, f32[1536,3,64]{0,2,1:T(8,128)}, u32[]{:S(2)}) copy-start(f32[1536,3,64]{0,2,1:T(8,128)} %get-tuple-element.453) | copy-start | bytes 3538948 | tf_op jit(solution)/shard_map/while
  262.7 3.8 copy-start.2
  262.7 4.0 copy-start.15
  266.3 7.7 %copy-start.7 = (f32[1536,3,64]{0,2,1:T(8,128)}, f32[1536,3,64]{0,2,1:T(8,128)S(1)}, u32[]{:S(2)}) copy-start(f32[1536,3,64]{0,2,1:T(8,128)S(1)} %fusion.123) | copy-start | bytes 3538948 | tf_op jit(solution)/shard_map/while
  269.1 4.9 copy-start.59
  274.0 7.2 %copy-start.58 = (s32[3]{0:T(128)}, s32[3]{0:T(128)S(1)}, u32[]{:S(2)}) copy-start(s32[3]{0:T(128)S(1)} %get-tuple-element.472) | copy-start | bytes 40 | tf_op jit(solution)/shard_map/while
  291.3 9.5 %copy-start.6 = (f32[1536,3,64]{0,2,1:T(8,128)S(1)}, f32[1536,3,64]{0,2,1:T(8,128)}, u32[]{:S(2)}) copy-start(f32[1536,3,64]{0,2,1:T(8,128)} %get-tuple-element.453) | copy-start | bytes 3538948 | tf_op jit(solution)/shard_map/while
  300.8 3.8 copy-start.2
  300.8 4.0 copy-start.15
  304.4 7.7 %copy-start.7 = (f32[1536,3,64]{0,2,1:T(8,128)}, f32[1536,3,64]{0,2,1:T(8,128)S(1)}, u32[]{:S(2)}) copy-start(f32[1536,3,64]{0,2,1:T(8,128)S(1)} %fusion.123) | copy-start | bytes 3538948 | tf_op jit(solution)/shard_map/while
  307.1 4.9 copy-start.59
  312.1 7.2 %copy-start.58 = (s32[3]{0:T(128)}, s32[3]{0:T(128)S(1)}, u32[]{:S(2)}) copy-start(s32[3]{0:T(128)S(1)} %get-tuple-element.472) | copy-start | bytes 40 | tf_op jit(solution)/shard_map/while
  329.4 9.5 %copy-start.6 = (f32[1536,3,64]{0,2,1:T(8,128)S(1)}, f32[1536,3,64]{0,2,1:T(8,128)}, u32[]{:S(2)}) copy-start(f32[1536,3,64]{0,2,1:T(8,128)} %get-tuple-element.453) | copy-start | bytes 3538948 | tf_op jit(solution)/shard_map/while
  338.9 3.8 copy-start.2
  338.9 4.0 copy-start.15
  342.4 7.7 %copy-start.7 = (f32[1536,3,64]{0,2,1:T(8,128)}, f32[1536,3,64]{0,2,1:T(8,128)S(1)}, u32[]{:S(2)}) copy-start(f32[1536,3,64]{0,2,1:T(8,128)S(1)} %fusion.123) | copy-start | bytes 3538948 | tf_op jit(solution)/shard_map/while
  345.2 4.9 copy-start.59
  358.8 5.7 copy-start.42
  358.8 239.0 %all-reduce.12.cloned.1.call-start = ((), (), s32[]{:S(2)}) async-start(), calls=%async_computation.2 | async-start | bytes 7077888 | tf_op jit(solution)/shard_map/psum | solution.py:183
  358.8 5.6 copy-start.19
  358.8 5.6 copy-start.63
  364.5 3.5 copy-start.21
  370.6 82.5 %copy-start.27 = (f32[1536]{0:T(1024)S(1)}, f32[1536]{0:T(1024)}, u32[]{:S(2)}) copy-start(f32[1536]{0:T(1024)} %copy-done.26) | copy-start | bytes 18436
  370.6 82.5 %copy-start.33 = (f32[768]{0:T(1024)S(1)}, f32[768]{0:T(1024)}, u32[]{:S(2)}) copy-start(f32[768]{0:T(1024)} %copy-done.32) | copy-start | bytes 9220
  372.0 85.8 %copy-start.37 = (f32[1536]{0:T(1024)S(1)}, f32[1536]{0:T(1024)}, u32[]{:S(2)}) copy-start(f32[1536]{0:T(1024)} %copy-done.36) | copy-start | bytes 18436
  372.0 85.9 %copy-start.29 = (f32[1536]{0:T(1024)S(1)}, f32[1536]{0:T(1024)}, u32[]{:S(2)}) copy-start(f32[1536]{0:T(1024)} %copy-done.28) | copy-start | bytes 18436
  453.1 4.8 copy-start.9
  457.8 4.5 copy-start.43
  457.8 4.4 copy-start.44
  457.8 4.4 copy-start.46
  457.8 4.4 copy-start.47
  457.8 4.4 copy-start.48
  457.9 49.8 %slice-start = ((s8[4718592]{0:T(1024)(128)(4,1)}), s8[524288]{0:T(1024)(128)(4,1)S(1)}, s32[]{:S(2)}) async-start(s8[4718592]{0:T(1024)(128)(4,1)} %bitcast.110), calls=%async_computation.4 | async-start | bytes 1048576
  502.9 4.9 slice-start.1
  502.9 5.9 copy-start.10
  597.8 5.8 copy-start.24
  597.8 8.1 %copy-start.1 = (bf16[768,768]{1,0:T(8,128)(2,1)S(1)}, bf16[768,768]{1,0:T(8,128)(2,1)}, u32[]{:S(2)}) copy-start(bf16[768,768]{1,0:T(8,128)(2,1)} %param.32) | copy-start | bytes 3538948
  597.8 7.2 %copy-start.25 = (bf16[192,768]{1,0:T(8,128)(2,1)S(1)}, bf16[192,768]{1,0:T(8,128)(2,1)}, u32[]{:S(2)}) copy-start(bf16[192,768]{1,0:T(8,128)(2,1)} %get-tuple-element.231) | copy-start | bytes 884740
  (26 other events, 49.5 us)
Sparse Core Ops, SparseCore 0:
  72.3 58.3 all-reduce.7
  159.2 55.7 all-reduce.9
  358.9 94.1 all-reduce.13
  458.0 139.6 all-reduce.11

commit v2 on v0

v2 whole, which is shorter than its diff:
```python
import functools

import jax
import jax.numpy as jnp
from jax import lax
from jax.experimental import pallas as pl
from jax.experimental.pallas import tpu as pltpu
from jax.sharding import PartitionSpec as P

HEAD_DIM = 64
NORM_EPS = 1e-06
MASK_FILL = -1e30
LOG2E = 1.4426950408889634
BLK = 128
COORDS = 64
f32 = jnp.float32
bf16 = jnp.bfloat16


def mm(a, b):
    return lax.dot_general(a, b, (((1,), (0,)), ((), ())), preferred_element_type=f32)


def mm_nt(a, b):
    return lax.dot_general(a, b, (((1,), (1,)), ((), ())), preferred_element_type=f32)


def mm_tn(a, b):
    return lax.dot_general(a, b, (((0,), (0,)), ((), ())), preferred_element_type=f32)


def norm_parts(v):
    width = v.shape[-1]
    mean = jnp.sum(v, axis=-1, keepdims=True) * (1.0 / width)
    centred = v - mean
    spread = jnp.sum(centred * centred, axis=-1, keepdims=True) * (1.0 / width)
    r = lax.rsqrt(spread + NORM_EPS)
    return centred * r, r


def norm_back(u, gain, x_hat, r):
    width = u.shape[-1]
    ug = u * gain
    m1 = jnp.sum(ug, axis=-1, keepdims=True) * (1.0 / width)
    m2 = jnp.sum(ug * x_hat, axis=-1, keepdims=True) * (1.0 / width)
    return r * (ug - m1 - x_hat * m2)


def gelu_pair(v):
    phi = 0.5 * (1.0 + lax.erf(v * 0.7071067811865476))
    dens = jnp.exp(-0.5 * v * v) * 0.3989422804014327
    return v * phi, phi + v * dens


class Sems:
    def __init__(self):
        self.count = 0
        self.ready_count = 0
        self.ready = None
        self.send = None
        self.recv = None

    def take(self, n=1):
        first = self.count
        self.count += n
        return first


def remote(sems, idx, src, dst, target):
    return pltpu.make_async_remote_copy(
        src_ref=src,
        dst_ref=dst,
        send_sem=sems.send.at[idx],
        recv_sem=sems.recv.at[idx],
        device_id=target,
        device_id_type=pl.DeviceIdType.MESH,
    )


class Gather:
    def __init__(self, sems, parts, view, t):
        self.sems, self.view, self.t = sems, view, t
        self.base = sems.take(3 * parts)
        self.parts = parts
        self.sib = t + 1 - 2 * lax.rem(t, 2)
        self.opp = lax.rem(t + 2, 4)

    def copy(self, kind, s, owner):
        ref = self.view(s, owner)
        target = {"tensor": self.opp if kind == 1 else self.sib}
        return remote(self.sems, self.base + kind * self.parts + s, ref, ref, target)

    def start(self, s):
        self.copy(1, s, self.t).start()
        self.copy(0, s, self.t).start()

    def forward(self, s):
        self.copy(1, s, self.opp).wait_recv()
        self.copy(2, s, self.opp).start()

    def finish(self, s):
        self.copy(0, s, self.sib).wait_recv()
        self.copy(2, s, lax.rem(self.sib + 2, 4)).wait_recv()
        self.copy(0, s, self.t).wait_send()
        self.copy(1, s, self.t).wait_send()
        self.copy(2, s, self.opp).wait_send()


class Scatter:
    def __init__(self, sems, parts, bufs, t):
        self.part, self.got_a, self.got_b = bufs
        self.sems = sems
        self.base = sems.take(2 * parts)
        self.parts = parts
        self.core = lax.rem(t, 2)
        self.chip = t // 2
        self.sib = t + 1 - 2 * lax.rem(t, 2)
        self.opp = lax.rem(t + 2, 4)

    def store(self, s, value):
        for o in range(4):
            self.part[s, o % 2, o // 2] = value[o * BLK : (o + 1) * BLK].astype(bf16)

    def copy_a(self, s):
        return remote(
            self.sems, self.base + s, self.part.at[s, 1 - self.core], self.got_a.at[s], {"tensor": self.sib}
        )

    def copy_b(self, s):
        return remote(
            self.sems,
            self.base + self.parts + s,
            self.part.at[s, self.core, 1 - self.chip],
            self.got_b.at[s],
            {"tensor": self.opp},
        )

    def start(self, s):
        self.copy_a(s).start()

    def across(self, s):
        self.copy_a(s).wait()
        other = 1 - self.chip
        self.part[s, self.core, other] = (
            self.part[s, self.core, other].astype(f32) + self.got_a[s, other].astype(f32)
        ).astype(bf16)
        self.copy_b(s).start()

    def finish(self, s):
        self.copy_b(s).wait()
        return (
            self.part[s, self.core, self.chip].astype(f32)
            + self.got_a[s, self.chip].astype(f32)
            + self.got_b[s].astype(f32)
        )


class Reduce:
    def __init__(self, sems, ref, got, rows, cols, halvings, order, dp, log_n):
        self.sems, self.ref, self.got, self.cols = sems, ref, got, cols
        rest = [b for b in range(log_n) if b not in order[:halvings]]
        self.bits = list(order[:halvings]) + rest
        self.halvings = halvings
        self.dp = dp
        self.base = sems.take(len(self.bits) + halvings)
        self.ready = sems.ready_count
        sems.ready_count += halvings
        self.low, self.size, self.spot = [0], [rows], []
        at = 0
        for j, b in enumerate(self.bits):
            side = lax.rem(dp // (1 << b), 2)
            if j < halvings:
                half = self.size[-1] // 2
                self.low.append(self.low[-1] + side * half)
                self.size.append(half)
            else:
                self.low.append(self.low[-1])
                self.size.append(self.size[-1])
            self.spot.append(at)
            at += self.size[-1]

    @staticmethod
    def got_rows(rows, halvings, log_n):
        return sum(rows >> (j + 1) for j in range(halvings)) + (log_n - halvings) * (rows >> halvings)

    def partner(self, j):
        step = 1 << self.bits[j]
        return {"dp": self.dp + step * (1 - 2 * lax.rem(self.dp // step, 2))}

    def at(self, ref, low, size):
        if not isinstance(low, int):
            low = pl.multiple_of(low, 16)
        return ref.at[pl.ds(low, size), pl.ds(0, self.cols)]

    def copy_in(self, j):
        size = self.size[j + 1]
        if j < self.halvings:
            other = self.low[j] + self.low[j] + size - self.low[j + 1]
        else:
            other = self.low[j]
        return remote(
            self.sems,
            self.base + j,
            self.at(self.ref, other, size),
            self.at(self.got, self.spot[j], size),
            self.partner(j),
        )

    def copy_back(self, j):
        here = self.at(self.ref, self.low[j + 1], self.size[j + 1])
        return remote(self.sems, self.base + len(self.bits) + j, here, here, self.partner(j))

    def copy_home(self, j):
        size = self.size[j + 1]
        other = self.low[j] + self.low[j] + size - self.low[j + 1]
        here = self.at(self.ref, other, size)
        return remote(self.sems, self.base + len(self.bits) + j, here, here, self.partner(j))

    def begin(self, j):
        self.copy_in(j).start()

    def add(self, j):
        self.copy_in(j).wait()
        if j < self.halvings:
            pl.semaphore_signal(
                self.sems.ready.at[self.ready + j],
                inc=1,
                device_id=self.partner(j),
                device_id_type=pl.DeviceIdType.MESH,
            )
        mine = self.at(self.ref, self.low[j + 1], self.size[j + 1])
        theirs = self.at(self.got, self.spot[j], self.size[j + 1])
        mine[...] = (mine[...].astype(f32) + theirs[...].astype(f32)).astype(bf16)

    def give(self, j):
        pl.semaphore_wait(self.sems.ready.at[self.ready + j], 1)
        self.copy_back(j).start()

    def take(self, j):
        self.copy_back(j).wait_send()
        self.copy_home(j).wait_recv()

    def steps(self):
        out = [lambda: self.begin(0)]
        n = len(self.bits)
        for j in range(n):

            def step(j=j):
                self.add(j)
                if j + 1 < n:
                    self.begin(j + 1)
                else:
                    self.give(self.halvings - 1)

            out.append(step)
        for j in reversed(range(self.halvings)):

            def back(j=j):
                self.take(j)
                if j > 0:
                    self.give(j - 1)

            out.append(back)
        return out


def layer_kernel(
    geo,
    lens,
    x_in,
    og_in,
    coords,
    w_qkv,
    w_out_in,
    w_fc1_in,
    w_fc2_in,
    vecs,
    table,
    out_layer,
    out_input,
    out_fc2,
    out_fc1,
    out_wout,
    out_qkv,
    out_small,
    x_mg,
    tg,
    n1,
    q_t,
    k_t,
    v_t,
    rows3,
    probs,
    mix,
    linv,
    w_out,
    w_fc1,
    w_fc2,
    mid_own,
    n2_oi,
    act_ol,
    pg_dq,
    part0,
    got_a0,
    got_b0,
    part1,
    got_a1,
    got_b1,
    mg_own,
    do_t,
    delta,
    acc,
    g_fc2,
    g_fc1,
    g_wout,
    g_qkv,
    r_fc2,
    r_fc1,
    r_wout,
    r_qkv,
    segk,
    tab3,
    small,
    small_got,
    fc1_sums,
    send,
    recv,
    ready,
    local,
):
    parts, log_n, heads = geo
    size = 4 * BLK
    dp = lax.axis_index("dp")
    t = lax.axis_index("tensor")
    sib = t + 1 - 2 * lax.rem(t, 2)
    opp = lax.rem(t + 2, 4)
    width = x_mg.shape[1]
    hd = heads * HEAD_DIM

    sems = Sems()
    sems.send, sems.recv, sems.ready = send, recv, ready

    def part_rows(s):
        return pl.ds(pl.multiple_of(s * size, size), size)

    def own_rows(s, owner):
        return pl.ds(pl.multiple_of(s * size + owner * BLK, BLK), BLK)

    def slot_rows(s, owner):
        return pl.ds(pl.multiple_of(owner * (parts * BLK) + s * BLK, BLK), BLK)

    ag_w = Gather(sems, 1, lambda s, o: w_out.at[pl.ds(pl.multiple_of(o * hd, hd), hd)], t)
    ag_mix = Gather(sems, parts, lambda s, o: mix.at[s, pl.ds(pl.multiple_of(o * hd, hd), hd)], t)
    ag_mg = Gather(sems, parts, lambda s, o: x_mg.at[own_rows(s, o)], t)
    ag_out = Gather(sems, parts, lambda s, o: act_ol.at[slot_rows(s, o)], t)
    ag_in = Gather(sems, parts, lambda s, o: n2_oi.at[slot_rows(s, o)], t)
    rs_n2 = Scatter(sems, parts, (part0, got_a0, got_b0), t)
    rs_mlp = Scatter(sems, parts, (part1, got_a1, got_b1), t)
    rs_n1 = Scatter(sems, parts, (part0, got_a0, got_b0), t)
    dp_fc2 = Reduce(sems, g_fc2, r_fc2, width, width, 3, (0, 1, 2), dp, log_n)
    dp_fc1 = Reduce(sems, g_fc1, r_fc1, width, width, 3, (0, 1, 2), dp, log_n)
    dp_wout = Reduce(sems, g_wout, r_wout, hd, width, 2, (1, 0), dp, log_n)
    dp_qkv = Reduce(sems, g_qkv, r_qkv, width, 3 * hd, 3, (0, 1, 2), dp, log_n)
    small_base = sems.take(2 + log_n)

    n_local = [0]
    pending = []

    def fetch(src, dst):
        cp = pltpu.make_async_copy(src, dst, local.at[n_local[0]])
        n_local[0] += 1
        cp.start()
        return cp

    x_loads = [
        [fetch(x_in.at[slot_rows(s, o)], x_mg.at[own_rows(s, o)]) for o in range(4)] for s in range(parts)
    ]
    w_out_load = fetch(w_out_in, w_out.at[pl.ds(pl.multiple_of(t * hd, hd), hd)])
    fc1_load = fetch(w_fc1_in, w_fc1)
    fc2_load = fetch(w_fc2_in, w_fc2)
    tg_loads = [
        fetch(og_in.at[slot_rows(s, o)], tg.at[own_rows(s, o)]) for s in range(parts) for o in range(4)
    ]

    barrier = pltpu.get_barrier_semaphore()
    for target in (sib, opp):
        pl.semaphore_signal(
            barrier, inc=1, device_id={"tensor": target}, device_id_type=pl.DeviceIdType.MESH
        )
    for b in range(log_n):
        step = 1 << b
        other = dp + step * (1 - 2 * lax.rem(dp // step, 2))
        pl.semaphore_signal(
            barrier, inc=1, device_id={"dp": other}, device_id_type=pl.DeviceIdType.MESH
        )
    pl.semaphore_wait(barrier, 2 + log_n)

    w_out_load.wait()
    ag_w.start(0)

    whole = table[...]
    hi = whole.astype(bf16)
    rest = whole - hi.astype(f32)
    mi = rest.astype(bf16)
    tab3[pl.ds(0, COORDS)] = hi
    tab3[pl.ds(COORDS, COORDS)] = mi
    tab3[pl.ds(2 * COORDS, COORDS)] = (rest - mi.astype(f32)).astype(bf16)

    ln1_gain, ln1_shift = vecs[0:1, :], vecs[1:2, :]
    ln2_gain, ln2_shift = vecs[2:3, :], vecs[3:4, :]
    b_out, b_fc2, b_fc1 = vecs[4:5, :], vecs[5:6, :], vecs[6:7, :]
    b_q, b_v = vecs[7:8, :hd], vecs[8:9, :hd]

    ends, total = [], 0
    for i in range(lens.shape[0]):
        total = total + lens[i]
        ends.append(total)

    def segment_of(place):
        passed = jnp.zeros_like(place)
        for e in ends:
            passed = passed + jnp.where(place >= e, 1, 0)
        return jnp.where(place < ends[-1], passed, len(ends) + place)

    def positions(rows_of, c):
        n = c.shape[1]
        values = lax.broadcasted_iota(jnp.int32, (COORDS, n), 0)
        cols = []
        for i in range(3):
            hot = jnp.where(values == c[i : i + 1, :], 1.0, 0.0).astype(bf16)
            cols.append(mm_tn(jnp.concatenate([hot, hot, hot], axis=0), tab3[...]))
        return jnp.concatenate(cols, axis=1)

    def lane_blocks(ref, s):
        return jnp.concatenate([ref[:, slot_rows(s, o)] for o in range(4)], axis=1)

    def hidden_of(s):
        return x_mg[part_rows(s), :].astype(f32) + positions(None, lane_blocks(coords, s))

    for s in range(parts):
        for cp in x_loads[s]:
            cp.wait()

    def project(s, carry):
        for o in range(4):
            place = lax.broadcasted_iota(jnp.int32, (BLK, BLK), 0) + (o * parts * BLK + s * BLK)
            segk[own_rows(s, o), :] = segment_of(place)
        x_hat, _ = norm_parts(hidden_of(s))
        low = (x_hat * ln1_gain + ln1_shift).astype(bf16)
        n1[part_rows(s), :] = low
        proj = mm(low, w_qkv[...])
        q = (proj[:, :hd] + b_q).astype(bf16).astype(f32).T.astype(bf16)
        k = proj[:, hd : 2 * hd].astype(bf16).astype(f32).T.astype(bf16)
        v = (proj[:, 2 * hd :] + b_v).astype(bf16).astype(f32).T.astype(bf16)
        for h in range(heads):
            head = slice(h * HEAD_DIM, (h + 1) * HEAD_DIM)
            q_t[h, :, part_rows(s)] = q[head]
            k_t[h, :, part_rows(s)] = k[head]
            v_t[h, :, part_rows(s)] = v[head]
            rows3[h, part_rows(s), :] = k[head].astype(f32).T.astype(bf16)
        return carry

    lax.fori_loop(0, parts, project, 0)

    def attend(s, carry):
        place = jnp.concatenate(
            [
                lax.broadcasted_iota(jnp.int32, (1, BLK), 1) + (o * parts * BLK + s * BLK)
                for o in range(4)
            ],
            axis=1,
        )
        allowed = segk[...][:, :1] == segment_of(place)
        for h in range(heads):
            scores = mm(rows3[h], q_t[h, :, part_rows(s)])
            scores = jnp.where(allowed, scores * (LOG2E / HEAD_DIM**0.5), MASK_FILL)
            top = jnp.max(scores, axis=0, keepdims=True)
            raised = jnp.exp2(scores - top)
            inv = 1.0 / jnp.sum(raised, axis=0, keepdims=True)
            low = raised.astype(bf16)
            probs[h, :, part_rows(s)] = low
            linv[h, :, part_rows(s)] = inv
            mixed = mm(v_t[h], low) * inv
            mix[s, pl.ds(pl.multiple_of(t * hd + h * HEAD_DIM, HEAD_DIM), HEAD_DIM), :] = mixed.astype(bf16)
        ag_mix.start(s)

        @pl.when(s >= 1)
        def _():
            ag_mix.forward(s - 1)

        return carry

    lax.fori_loop(0, parts, attend, 0)
    ag_w.forward(0)
    for cp in tg_loads:
        cp.wait()
    fc1_load.wait()
    fc2_load.wait()
    ag_w.finish(0)
    fc1_sums[...] = jnp.zeros_like(fc1_sums)
    small[0] = jnp.zeros_like(small[0])

    def visible_rows(s, owner):
        return segk[own_rows(s, owner), :][:, :1] < len(ends)

    def second_norm_back(s):
        u = rs_n2.finish(s)
        middle = mid_own[s]
        x_hat, r = norm_parts(middle)
        grad = tg[own_rows(s, t), :].astype(f32) + norm_back(u, ln2_gain, x_hat, r)
        mg_own[s] = grad
        small[0, 2:3, :] += jnp.sum(u * x_hat, axis=0, keepdims=True)
        small[0, 3:4, :] += jnp.sum(u, axis=0, keepdims=True)
        small[0, 4:5, :] += jnp.sum(grad, axis=0, keepdims=True)
        small[0, 5:6, :] += jnp.sum(tg[own_rows(s, t), :].astype(f32), axis=0, keepdims=True)
        x_mg[own_rows(s, t), :] = grad.astype(bf16)
        ag_mg.start(s)

    def feed(s, carry):
        @pl.when(s == parts - 1)
        def _():
            ag_mix.forward(s)

        ag_mix.finish(s)
        attn = mm_tn(mix[s], w_out[...])
        middle = hidden_of(s) + attn + b_out
        mine = middle[:BLK]
        for o in range(1, 4):
            mine = jnp.where(t == o, middle[o * BLK : (o + 1) * BLK], mine)
        mid_own[s] = mine
        x_hat, _ = norm_parts(middle)
        low = (x_hat * ln2_gain + ln2_shift).astype(bf16)
        n2_oi[part_rows(s), :] = low
        value, slope = gelu_pair(mm(low, w_fc1[...]) + b_fc1)
        act_ol[part_rows(s), :] = value.astype(bf16)
        shown = segk[part_rows(s), :][:, :1] < len(ends)
        top = jnp.where(shown, tg[part_rows(s), :].astype(f32), 0.0).astype(bf16)
        tg[part_rows(s), :] = top
        pre = (mm_nt(top, w_fc2[...]) * slope).astype(bf16)
        pg_dq[part_rows(s), :] = pre
        fc1_sums[0:1, :] += jnp.sum(pre.astype(f32), axis=0, keepdims=True)
        rs_n2.store(s, mm_nt(pre, w_fc1[...]))
        rs_n2.start(s)

        @pl.when(s >= 1)
        def _():
            second_norm_back(s - 1)

        @pl.when(s >= 2)
        def _():
            ag_mg.forward(s - 2)

        rs_mlp.store(s, mm(act_ol[part_rows(s), :], w_fc2[...]))
        rs_n2.across(s)
        return carry

    lax.fori_loop(0, parts, feed, 0)

    def weight_grad(dst, left, right, cols):
        for i in range(left.shape[1] // 256):
            dst[i * 256 : (i + 1) * 256, :cols] = mm_tn(left[:, i * 256 : (i + 1) * 256], right[:, :cols]).astype(bf16)

    s_fc2, s_fc1, s_wout, s_qkv = dp_fc2.steps(), dp_fc1.steps(), dp_wout.steps(), dp_qkv.steps()

    def go(steps, n=1):
        for _ in range(n):
            if steps:
                steps.pop(0)()

    weight_grad(g_fc2, act_ol, tg, width)
    go(s_fc2)
    second_norm_back(parts - 1)
    x_own_loads = [fetch(x_in.at[slot_rows(s, t)], tg.at[own_rows(s, t)]) for s in range(parts)]
    if parts >= 2:
        ag_mg.forward(parts - 2)
    weight_grad(g_fc1, n2_oi, pg_dq, width)
    go(s_fc1)
    ag_mg.forward(parts - 1)
    for s in range(parts):
        ag_mg.finish(s)
    for s in range(parts):
        rs_mlp.start(s)

    for s in range(parts):
        rows = part_rows(s)
        own = pl.ds(pl.multiple_of(t * hd, hd), hd)
        low = mm_nt(x_mg[rows, :], w_out[own, :]).astype(bf16).astype(f32).T
        for h in range(heads):
            scaled = (low[h * HEAD_DIM : (h + 1) * HEAD_DIM] * linv[h, :, rows]).astype(bf16)
            do_t[h, :, rows] = scaled
            mixed = mix[s, pl.ds(pl.multiple_of(t * hd + h * HEAD_DIM, HEAD_DIM), HEAD_DIM), :]
            delta[h, :, rows] = jnp.sum(scaled.astype(f32) * mixed.astype(f32), axis=0, keepdims=True)
    for s in range(parts):
        rs_mlp.across(s)
    own = pl.ds(pl.multiple_of(t * hd, hd), hd)
    grad_out = mm(mix[0, own, :], x_mg[part_rows(0), :])
    for s in range(1, parts):
        grad_out = grad_out + mm(mix[s, own, :], x_mg[part_rows(s), :])
    g_wout[...] = grad_out.astype(bf16)
    go(s_wout)

    for h in range(heads):
        rows3[0] = v_t[h].astype(f32).T.astype(bf16)
        rows3[1] = q_t[h].astype(f32).T.astype(bf16)
        rows3[2] = do_t[h].astype(f32).T.astype(bf16)

        def back(s, carry, h=h):
            rows = part_rows(s)
            p = probs[h, rows, :]
            wg = mm(rows3[0, rows, :], do_t[h])
            sg = (p.astype(f32) * (wg - delta[h])).astype(bf16)
            dv = mm(p, rows3[2])
            dk = mm(sg, rows3[1]) * (1.0 / HEAD_DIM**0.5)
            pg_dq[rows, hd + h * HEAD_DIM : hd + (h + 1) * HEAD_DIM] = dk.astype(bf16)
            pg_dq[rows, 2 * hd + h * HEAD_DIM : 2 * hd + (h + 1) * HEAD_DIM] = dv.astype(bf16)
            dq = mm(k_t[h, :, rows], sg)

            @pl.when(s == 0)
            def _():
                acc[...] = dq

            @pl.when(s > 0)
            def _():
                acc[...] += dq

            return carry

        lax.fori_loop(0, parts, back, 0)
        pg_dq[:, h * HEAD_DIM : (h + 1) * HEAD_DIM] = (acc[...].T * (1.0 / HEAD_DIM**0.5)).astype(bf16)
        go(s_fc2)
        go(s_fc1)
        if h == 1:
            go(s_wout)

    for s in range(parts):
        rs_n1.store(s, mm_nt(pg_dq[part_rows(s), : 3 * hd], w_qkv[...]))
        rs_n1.start(s)
        if s >= 1:
            rs_n1.across(s - 1)
    weight_grad(g_qkv, n1, pg_dq, 3 * hd)
    rs_n1.across(parts - 1)
    go(s_qkv)
    sums = jnp.sum(pg_dq[:, : 3 * hd].astype(f32), axis=0, keepdims=True)
    small[0, 8:9, :] = fc1_sums[0:1, :]
    small[0, 9:10, :hd] = sums[:, :hd]
    small[0, 10:11, :hd] = sums[:, 2 * hd :]

    def first_norm_back(s):
        u = rs_n1.finish(s)
        hidden = tg[own_rows(s, t), :].astype(f32) + positions(None, coords[:, slot_rows(s, t)])
        x_hat, r = norm_parts(hidden)
        grad = mg_own[s] + norm_back(u, ln1_gain, x_hat, r)
        small[0, 0:1, :] += jnp.sum(u * x_hat, axis=0, keepdims=True)
        small[0, 1:2, :] += jnp.sum(u, axis=0, keepdims=True)
        n2_oi[slot_rows(s, t), :] = grad.astype(bf16)
        ag_in.start(s)

    for cp in x_own_loads:
        cp.wait()
    for s in range(parts):
        first_norm_back(s)
        if s >= 1:
            ag_in.forward(s - 1)
        go(s_fc2)
        go(s_fc1)
        go(s_wout)
        go(s_qkv)

    def layer_out(s):
        total = mid_own[s] + rs_mlp.finish(s) + b_fc2
        act_ol[slot_rows(s, t), :] = jnp.where(visible_rows(s, t), total, 0.0).astype(bf16)
        ag_out.start(s)

    for s in range(parts):
        layer_out(s)
    ag_in.forward(parts - 1)

    def small_copy(i, rows, target):
        return remote(
            sems, small_base + i, small.at[i, pl.ds(0, rows)], small_got.at[i, pl.ds(0, rows)], target
        )

    hops = [(8, {"tensor": sib}), (8, {"tensor": opp})]
    for b in range(log_n):
        step = 1 << b
        hops.append((16, {"dp": dp + step * (1 - 2 * lax.rem(dp // step, 2))}))
    for i, (rows, target) in enumerate(hops):
        cp = small_copy(i, rows, target)
        cp.start()
        cp.wait()
        small[i + 1, 0:rows] = small[i, 0:rows] + small_got[i, 0:rows]
        if rows < 16:
            small[i + 1, rows:16] = small[i, rows:16]
        go(s_qkv)
        go(s_fc2)
        go(s_fc1)
        go(s_wout)

    outs = []
    for steps, ref, dst in (
        (s_fc2, g_fc2, out_fc2),
        (s_fc1, g_fc1, out_fc1),
        (s_wout, g_wout, out_wout),
    ):
        go(steps, len(steps))
        outs.append(fetch(ref, dst))
    outs.append(fetch(small.at[len(hops)], out_small))
    for s in range(parts):
        ag_in.finish(s)
    outs.append(fetch(n2_oi, out_input))
    for s in range(parts):
        ag_out.forward(s)
    for s in range(parts):
        ag_out.finish(s)
    outs.append(fetch(act_ol, out_layer))
    go(s_qkv, len(s_qkv))
    outs.append(fetch(g_qkv, out_qkv))
    for cp in outs:
        cp.wait()


def sincos_rows(feature_count):
    half_width = feature_count // 6
    ladder = jnp.arange(half_width, dtype=f32) / half_width
    frequency = jnp.power(10000.0, -ladder)
    angles = jnp.arange(COORDS, dtype=jnp.int32).astype(f32)[:, None] * frequency[None, :]
    return jnp.concatenate([jnp.sin(angles), jnp.cos(angles)], axis=1)


def on_device(
    n_dp,
    layer_input,
    patch_coords,
    item_lengths,
    out_grad,
    ln1_gain,
    ln1_shift,
    w_qkv,
    b_qv,
    w_out,
    b_out,
    ln2_gain,
    ln2_shift,
    w_fc1,
    b_fc1,
    w_fc2,
    b_fc2,
):
    tokens, width = layer_input.shape
    hd = w_out.shape[0]
    ff = w_fc1.shape[1]
    heads = hd // HEAD_DIM
    parts = tokens // (4 * BLK)
    log_n = n_dp.bit_length() - 1
    size = 4 * BLK
    pad = lambda v: jnp.pad(v, (0, width - v.shape[0]))
    vecs = jnp.stack(
        [
            pad(v.astype(f32))
            for v in (ln1_gain, ln1_shift, ln2_gain, ln2_shift, b_out, b_fc2, b_fc1, b_qv[0], b_qv[1])
        ]
        + [jnp.zeros((width,), f32)] * 7
    )
    got = Reduce.got_rows
    vmem = lambda *s: pltpu.VMEM(s, bf16)
    vmem32 = lambda *s: pltpu.VMEM(s, f32)
    scratch = [
        vmem(tokens, width),
        vmem(tokens, width),
        vmem(tokens, width),
        vmem(heads, HEAD_DIM, tokens),
        vmem(heads, HEAD_DIM, tokens),
        vmem(heads, HEAD_DIM, tokens),
        vmem(heads, tokens, HEAD_DIM),
        vmem(heads, tokens, tokens),
        vmem(parts, 4 * hd, size),
        vmem32(heads, 1, tokens),
        vmem(4 * hd, width),
        vmem(width, ff),
        vmem(ff, width),
        vmem32(parts, BLK, width),
        vmem(tokens, width),
        vmem(tokens, width),
        vmem(tokens, width),
    ]
    for _ in range(2):
        scratch += [
            vmem(parts, 2, 2, BLK, width),
            vmem(parts, 2, BLK, width),
            vmem(parts, BLK, width),
        ]
    scratch += [
        vmem32(parts, BLK, width),
        vmem(heads, HEAD_DIM, tokens),
        vmem32(heads, 1, tokens),
        vmem32(HEAD_DIM, tokens),
        vmem(ff, width),
        vmem(width, ff),
        vmem(hd, width),
        vmem(width, 3 * hd),
        vmem(got(ff, 3, log_n), width),
        vmem(got(width, 3, log_n), width),
        vmem(got(hd, 2, log_n), width),
        vmem(got(width, 3, log_n), 3 * hd),
        pltpu.VMEM((tokens, BLK), jnp.int32),
        vmem(3 * COORDS, 2 * (width // 6)),
        vmem32(3 + log_n, 16, width),
        vmem32(2 + log_n, 16, width),
        vmem32(8, ff),
    ]
    n_sems = 3 + 4 * 3 * parts + 3 * 2 * parts + 3 * (log_n + 3) + (log_n + 2) + 2 + log_n
    scratch += [
        pltpu.SemaphoreType.DMA((n_sems,)),
        pltpu.SemaphoreType.DMA((n_sems,)),
        pltpu.SemaphoreType.REGULAR((11,)),
        pltpu.SemaphoreType.DMA((4 * parts * 2 + parts + 3 + 7,)),
    ]
    shape = jax.ShapeDtypeStruct
    hbm = pl.BlockSpec(memory_space=pl.ANY)
    here = pl.BlockSpec(memory_space=pltpu.VMEM)
    results = pl.pallas_call(
        functools.partial(layer_kernel, (parts, log_n, heads)),
        name="layer",
        out_shape=(
            shape((tokens, width), bf16),
            shape((tokens, width), bf16),
            shape((ff, width), bf16),
            shape((width, ff), bf16),
            shape((hd, width), bf16),
            shape((width, 3 * hd), bf16),
            shape((16, width), f32),
        ),
        in_specs=[pl.BlockSpec(memory_space=pltpu.SMEM), hbm, hbm, here, here, hbm, hbm, hbm, here, here],
        out_specs=(hbm,) * 7,
        scratch_shapes=scratch,
        compiler_params=pltpu.CompilerParams(
            collective_id=0, has_side_effects=True, vmem_limit_bytes=67043328
        ),
    )(
        item_lengths,
        layer_input,
        out_grad,
        patch_coords,
        w_qkv.reshape(width, 3 * hd),
        w_out,
        w_fc1,
        w_fc2,
        vecs,
        sincos_rows(width),
    )
    layer_output, input_grad, g_fc2, g_fc1, g_wout, g_qkv, small = results
    return (
        layer_output,
        input_grad.astype(f32),
        small[0],
        small[1],
        g_qkv.astype(f32).reshape(width, 3, hd),
        small[9:11, :hd],
        g_wout.astype(f32),
        small[4],
        small[2],
        small[3],
        g_fc1.astype(f32),
        small[8, :ff],
        g_fc2.astype(f32),
        small[5],
    )


def solution(mesh):
    placed = (
        P("dp", None),
        P(None, "dp"),
        P("dp"),
        P("dp", None),
        P(),
        P(),
        P(None, None, "tensor"),
        P(None, "tensor"),
        P("tensor", None),
        P(),
        P(),
        P(),
        P(None, "tensor"),
        P("tensor"),
        P("tensor", None),
        P(),
    )
    return jax.shard_map(
        functools.partial(on_device, mesh.shape["dp"]),
        mesh=mesh,
        in_specs=placed,
        out_specs=(
            P("dp", None),
            P("dp", None),
            P(),
            P(),
            P(None, None, "tensor"),
            P(None, "tensor"),
            P("tensor", None),
            P(),
            P(),
            P(),
            P(None, "tensor"),
            P("tensor"),
            P("tensor", None),
            P(),
        ),
        check_vma=False,
    )
```

time: 928 us -> 218 us (0.23)
  waiting for transfers between devices: 439 us -> 0 us
  matrix products: 196 us -> 0 us
  Pallas kernels: 0 us -> 192 us
  other arithmetic: 176 us -> 9.16 us
  blocking collectives: 38.4 us -> 0 us
  local copies, waits for them, and re-layouts: 47.8 us -> 15.9 us
  between operations: 15.2 us -> 0.73 us
    psum x6 -> x0, waiting for transfers between devices: 439 us -> none  [the longest x1 226 us: on_device(): lax.psum((grad_ln1_gain, grad_ln1_shift, grad_w_qkv, grad_b_qv, grad_w_ou...]
    pallas_call x0 -> x1, Pallas kernels: none -> 192 us  [on_device(): pl.pallas_call(functools.partial(layer_kernel, (parts, log_n, heads)), na...]
    dot_general x38 -> x0, matrix products: 188 us -> none  [the longest x9 42.9 us: block_scores(): jnp.einsum('qhd,khd->hqk', query_block, key_rows, preferred_element_type=...]
    reduce_sum x16 -> x0, other arithmetic: 54.2 us -> none  [the longest x4 21.1 us: layer_norm(): return centred * lax.rsqrt(spread + NORM_EPS) * norm_gain + norm_shift]
    sub x3 -> x0, other arithmetic: 42.9 us -> none  [attend_block(): raised = jnp.exp(scores - row_max)]
    psum x1 -> x0, blocking collectives: 38.4 us -> none  [on_device(): lax.psum((grad_ln1_gain, grad_ln1_shift, grad_w_qkv, grad_b_qv, grad_w_ou...]
    convert_element_type x16 -> x5, other arithmetic: 41.1 us -> 8.3 us  [the longest x1 4.29 us: on_device(): input_grad.astype(f32)]
    dynamic_slice x18 -> x0, local copies, waits for them, and re-layouts: 15.7 us -> none  [the longest x6 6.24 us: attend_block(): lax.dynamic_slice_in_dim(segment, block_start, block_rows, 0)]
  transfers between devices with their start and end apart: 6 -> 0, of which waited for: 5 -> 0; matrix products, arithmetic and copies ran while one was open for 4% -> 0% of each run, Pallas kernels for 0% -> 0%
where the time goes in v2:
time: 218 us
  Pallas kernels  192 us (88%)
  local copies, waits for them, and re-layouts  15.9 us (7%)
  other arithmetic  9.16 us (4%)
    pallas_call x1, Pallas kernels, on_device(): pl.pallas_call(functools.partial(layer_kernel, (parts, log_n, heads)), na...  192 us
    another operation x13, local copies, waits for them, and re-layouts, on_device(): jnp.stack([pad(v.astype(f32)) for v in (ln1_gain, ln1_shift, ln2_gain, ln...  6.09 us

profile of v2, /device:TPU:0, one launch (start us, length us, event | category | flops | bytes accessed | tf_op | source)
XLA Modules:
  0.0 218.0 jit_solution(17494867847861776048)
XLA Ops:
  0.6 2.2 %copy.32.w_qkv = bf16[768,576]{1,0:T(8,128)(2,1)} copy(bf16[768,576]{0,1:T(8,128)(2,1)} %bitcast.3) | data formatting | bytes 1769472 | tf_op jit(solution)/shard_map/reshape | solution.py:844
  2.9 0.7 reshape.54
  3.6 0.7 reshape.55
  4.2 0.7 reshape.56
  4.9 0.7 reshape.57
  5.6 0.7 reshape.58
  6.3 0.7 reshape.59
  7.0 0.7 reshape.60
  7.7 0.8 slice_reduce_fusion.7
  8.5 1.3 stack.83.vecs
  9.8 0.2 multiply_sine_fusion
  10.0 0.6 pad_maximum_fusion.table
  10.6 192.1 %layer.1 = (bf16[1536,768]{1,0:T(8,128)(2,1)}, bf16[1536,768]{1,0:T(8,128)(2,1)}, bf16[768,768]{1,0:T(8,128)(2,1)}, bf16[768,768]{1,0:T(8,128)(2,1)}, bf16[192,7...) custom-call(s32[4]{0:T(128)} %lens.1, bf16[1536,768]{1,0:T(8,128)(2,1)} %x_in.1, ...), custom_call_target="tpu_custom_call" | custom-call | tf_op jit(solution)/shard_map/layer/pallas_call | solution.py:821
  202.8 0.0 copy-start.3
  202.8 4.3 %convert_element_type.43 = f32[1536,768]{1,0:T(8,128)} convert(bf16[1536,768]{1,0:T(8,128)(2,1)} %get-tuple-element.22) | non-fusion elementwise | flops 1179648 | bytes 7077888 | tf_op jit(solution)/shard_map/convert_element_type | solution.py:854
  207.1 0.0 copy-start.4
  207.1 0.0 copy-start.2
  207.1 1.6 slice_reduce_fusion
  208.7 0.0 copy-done.3
  208.7 1.5 copy.33
  210.2 0.0 copy-start.1
  210.2 1.4 slice.34
  211.6 0.0 copy-done.4
  211.6 0.9 convert_element_type.44
  212.5 0.0 copy-done.2
  212.5 1.6 convert_element_type.45
  214.0 0.0 copy-start
  214.0 0.0 copy-done.1
  214.0 1.6 convert_element_type.46
  215.6 0.9 copy-done
  216.6 1.4 copy.35
  (8 shorter events, 0.0 us)
Async XLA Ops:
  202.8 5.9 %copy-start.3 = (bf16[768,576]{1,0:T(8,128)(2,1)S(1)}, bf16[768,576]{1,0:T(8,128)(2,1)}, u32[]{:S(2)}) copy-start(bf16[768,576]{1,0:T(8,128)(2,1)} %get-tuple-element.24) | copy-start | bytes 2654212
  207.1 4.5 %copy-start.4 = (bf16[192,768]{1,0:T(8,128)(2,1)S(1)}, bf16[192,768]{1,0:T(8,128)(2,1)}, u32[]{:S(2)}) copy-start(bf16[192,768]{1,0:T(8,128)(2,1)} %get-tuple-element.25) | copy-start | bytes 884740
  207.1 5.4 %copy-start.2 = (bf16[768,768]{1,0:T(8,128)(2,1)S(1)}, bf16[768,768]{1,0:T(8,128)(2,1)}, u32[]{:S(2)}) copy-start(bf16[768,768]{1,0:T(8,128)(2,1)} %get-tuple-element.26) | copy-start | bytes 3538948
  210.2 3.8 %copy-start.1 = (bf16[768,768]{1,0:T(8,128)(2,1)S(1)}, bf16[768,768]{1,0:T(8,128)(2,1)}, u32[]{:S(2)}) copy-start(bf16[768,768]{1,0:T(8,128)(2,1)} %get-tuple-element.27) | copy-start | bytes 3538948
  214.0 2.5 %copy-start = (bf16[1536,768]{1,0:T(8,128)(2,1)S(1)}, bf16[1536,768]{1,0:T(8,128)(2,1)}, u32[]{:S(2)}) copy-start(bf16[1536,768]{1,0:T(8,128)(2,1)} %get-tuple-element.69) | copy-start | bytes 7077892

commit v3 on v2

--- a/solution.py
+++ b/solution.py
@@ -2,6 +2,8 @@
 
 import jax
 import jax.numpy as jnp
+import ml_dtypes
+import numpy as np
 from jax import lax
 from jax.experimental import pallas as pl
 from jax.experimental.pallas import tpu as pltpu
@@ -156,7 +158,7 @@
 
 
 class Reduce:
-    def __init__(self, sems, ref, got, rows, cols, halvings, order, dp, log_n):
+    def __init__(self, sems, ref, got, rows, cols, halvings, order, dp, log_n, first=0):
         self.sems, self.ref, self.got, self.cols = sems, ref, got, cols
         rest = [b for b in range(log_n) if b not in order[:halvings]]
         self.bits = list(order[:halvings]) + rest
@@ -165,7 +167,7 @@
         self.base = sems.take(len(self.bits) + halvings)
         self.ready = sems.ready_count
         sems.ready_count += halvings
-        self.low, self.size, self.spot = [0], [rows], []
+        self.low, self.size, self.spot = [first], [rows], []
         at = 0
         for j, b in enumerate(self.bits):
             side = lax.rem(dp // (1 << b), 2)
@@ -274,8 +276,15 @@
     w_out_in,
     w_fc1_in,
     w_fc2_in,
-    vecs,
-    table,
+    v0,
+    v1,
+    v2,
+    v3,
+    v4,
+    v5,
+    v6,
+    b_qv,
+    tab3,
     out_layer,
     out_input,
     out_fc2,
@@ -317,9 +326,9 @@
     r_fc2,
     r_fc1,
     r_wout,
-    r_qkv,
+    r_qa,
+    r_qb,
     segk,
-    tab3,
     small,
     small_got,
     fc1_sums,
@@ -329,6 +338,7 @@
     local,
 ):
     parts, log_n, heads = geo
+    vecs = (v0, v1, v2, v3, v4, v5, v6)
     size = 4 * BLK
     dp = lax.axis_index("dp")
     t = lax.axis_index("tensor")
@@ -358,9 +368,11 @@
     rs_mlp = Scatter(sems, parts, (part1, got_a1, got_b1), t)
     rs_n1 = Scatter(sems, parts, (part0, got_a0, got_b0), t)
     dp_fc2 = Reduce(sems, g_fc2, r_fc2, width, width, 3, (0, 1, 2), dp, log_n)
-    dp_fc1 = Reduce(sems, g_fc1, r_fc1, width, width, 3, (0, 1, 2), dp, log_n)
+    dp_fc1 = Reduce(sems, g_fc1, r_fc1, width, width, 3, (1, 0, 2), dp, log_n)
     dp_wout = Reduce(sems, g_wout, r_wout, hd, width, 2, (1, 0), dp, log_n)
-    dp_qkv = Reduce(sems, g_qkv, r_qkv, width, 3 * hd, 3, (0, 1, 2), dp, log_n)
+    half = width // 2
+    dp_qa = Reduce(sems, g_qkv, r_qa, half, 3 * hd, 3, (0, 1, 2), dp, log_n)
+    dp_qb = Reduce(sems, g_qkv, r_qb, half, 3 * hd, 3, (1, 0, 2), dp, log_n, half)
     small_base = sems.take(2 + log_n)
 
     n_local = [0]
@@ -398,18 +410,11 @@
     w_out_load.wait()
     ag_w.start(0)
 
-    whole = table[...]
-    hi = whole.astype(bf16)
-    rest = whole - hi.astype(f32)
-    mi = rest.astype(bf16)
-    tab3[pl.ds(0, COORDS)] = hi
-    tab3[pl.ds(COORDS, COORDS)] = mi
-    tab3[pl.ds(2 * COORDS, COORDS)] = (rest - mi.astype(f32)).astype(bf16)
-
-    ln1_gain, ln1_shift = vecs[0:1, :], vecs[1:2, :]
-    ln2_gain, ln2_shift = vecs[2:3, :], vecs[3:4, :]
-    b_out, b_fc2, b_fc1 = vecs[4:5, :], vecs[5:6, :], vecs[6:7, :]
-    b_q, b_v = vecs[7:8, :hd], vecs[8:9, :hd]
+    def row(ref):
+        return ref[...].astype(f32).reshape(1, ref.shape[0])
+
+    ln1_gain, ln1_shift, ln2_gain, ln2_shift, b_out, b_fc2, b_fc1 = [row(v) for v in vecs]
+    b_q, b_v = b_qv[0:1, :].astype(f32), b_qv[1:2, :].astype(f32)
 
     ends, total = [], 0
     for i in range(lens.shape[0]):
@@ -448,7 +453,7 @@
         x_hat, _ = norm_parts(hidden_of(s))
         low = (x_hat * ln1_gain + ln1_shift).astype(bf16)
         n1[part_rows(s), :] = low
-        proj = mm(low, w_qkv[...])
+        proj = mm_nt(low, w_qkv[...])
         q = (proj[:, :hd] + b_q).astype(bf16).astype(f32).T.astype(bf16)
         k = proj[:, hd : 2 * hd].astype(bf16).astype(f32).T.astype(bf16)
         v = (proj[:, 2 * hd :] + b_v).astype(bf16).astype(f32).T.astype(bf16)
@@ -556,30 +561,40 @@
 
     lax.fori_loop(0, parts, feed, 0)
 
-    def weight_grad(dst, left, right, cols):
-        for i in range(left.shape[1] // 256):
-            dst[i * 256 : (i + 1) * 256, :cols] = mm_tn(left[:, i * 256 : (i + 1) * 256], right[:, :cols]).astype(bf16)
-
-    s_fc2, s_fc1, s_wout, s_qkv = dp_fc2.steps(), dp_fc1.steps(), dp_wout.steps(), dp_qkv.steps()
-
-    def go(steps, n=1):
-        for _ in range(n):
+    def weight_grad(dst, left, right, cols, first=0, last=None):
+        last = left.shape[1] if last is None else last
+        for i in range(first, last, 256 if (last - first) % 256 == 0 else last - first):
+            n = 256 if (last - first) % 256 == 0 else last - first
+            dst[i : i + n, :cols] = mm_tn(left[:, i : i + n], right[:, :cols]).astype(bf16)
+
+    s_fc2, s_fc1, s_wout = dp_fc2.steps(), dp_fc1.steps(), dp_wout.steps()
+    s_qa, s_qb = dp_qa.steps(), dp_qb.steps()
+
+    def go(*chains):
+        for steps in chains:
             if steps:
                 steps.pop(0)()
 
     weight_grad(g_fc2, act_ol, tg, width)
     go(s_fc2)
+    for s in range(parts):
+        rs_mlp.start(s)
     second_norm_back(parts - 1)
     x_own_loads = [fetch(x_in.at[slot_rows(s, t)], tg.at[own_rows(s, t)]) for s in range(parts)]
     if parts >= 2:
         ag_mg.forward(parts - 2)
+    for s in range(parts):
+        rs_mlp.across(s)
     weight_grad(g_fc1, n2_oi, pg_dq, width)
     go(s_fc1)
     ag_mg.forward(parts - 1)
     for s in range(parts):
         ag_mg.finish(s)
-    for s in range(parts):
-        rs_mlp.start(s)
+
+    def layer_out(s):
+        total = mid_own[s] + rs_mlp.finish(s) + b_fc2
+        act_ol[slot_rows(s, t), :] = jnp.where(visible_rows(s, t), total, 0.0).astype(bf16)
+        ag_out.start(s)
 
     for s in range(parts):
         rows = part_rows(s)
@@ -590,8 +605,6 @@
             do_t[h, :, rows] = scaled
             mixed = mix[s, pl.ds(pl.multiple_of(t * hd + h * HEAD_DIM, HEAD_DIM), HEAD_DIM), :]
             delta[h, :, rows] = jnp.sum(scaled.astype(f32) * mixed.astype(f32), axis=0, keepdims=True)
-    for s in range(parts):
-        rs_mlp.across(s)
     own = pl.ds(pl.multiple_of(t * hd, hd), hd)
     grad_out = mm(mix[0, own, :], x_mg[part_rows(0), :])
     for s in range(1, parts):
@@ -627,19 +640,31 @@
 
         lax.fori_loop(0, parts, back, 0)
         pg_dq[:, h * HEAD_DIM : (h + 1) * HEAD_DIM] = (acc[...].T * (1.0 / HEAD_DIM**0.5)).astype(bf16)
-        go(s_fc2)
-        go(s_fc1)
+        go(s_fc2, s_fc1)
+        if h == 0:
+            layer_out(0)
         if h == 1:
             go(s_wout)
+            for s in range(1, parts):
+                layer_out(s)
+        if h == heads - 1:
+            go(s_wout)
+            for s in range(parts):
+                ag_out.forward(s)
 
     for s in range(parts):
-        rs_n1.store(s, mm_nt(pg_dq[part_rows(s), : 3 * hd], w_qkv[...]))
+        rs_n1.store(s, mm(pg_dq[part_rows(s), : 3 * hd], w_qkv[...]))
         rs_n1.start(s)
         if s >= 1:
             rs_n1.across(s - 1)
-    weight_grad(g_qkv, n1, pg_dq, 3 * hd)
+        if s == 0:
+            weight_grad(g_qkv, n1, pg_dq, 3 * hd, 0, half)
+            go(s_qa)
+        if s == 1:
+            weight_grad(g_qkv, n1, pg_dq, 3 * hd, half, width)
+            go(s_qb)
     rs_n1.across(parts - 1)
-    go(s_qkv)
+    go(s_fc2, s_fc1, s_wout)
     sums = jnp.sum(pg_dq[:, : 3 * hd].astype(f32), axis=0, keepdims=True)
     small[0, 8:9, :] = fc1_sums[0:1, :]
     small[0, 9:10, :hd] = sums[:, :hd]
@@ -655,76 +680,80 @@
         n2_oi[slot_rows(s, t), :] = grad.astype(bf16)
         ag_in.start(s)
 
+    hops = [(8, {"tensor": sib}), (8, {"tensor": opp})]
+    for b in range(log_n):
+        step = 1 << b
+        hops.append((16, {"dp": dp + step * (1 - 2 * lax.rem(dp // step, 2))}))
+
+    def small_copy(i):
+        rows, target = hops[i]
+        return remote(
+            sems, small_base + i, small.at[i, pl.ds(0, rows)], small_got.at[i, pl.ds(0, rows)], target
+        )
+
+    def small_add(i):
+        rows = hops[i][0]
+        small_copy(i).wait()
+        small[i + 1, 0:rows] = small[i, 0:rows] + small_got[i, 0:rows]
+        if rows < 16:
+            small[i + 1, rows:16] = small[i, rows:16]
+        if i + 1 < len(hops):
+            small_copy(i + 1).start()
+
     for cp in x_own_loads:
         cp.wait()
     for s in range(parts):
         first_norm_back(s)
         if s >= 1:
             ag_in.forward(s - 1)
-        go(s_fc2)
-        go(s_fc1)
-        go(s_wout)
-        go(s_qkv)
-
-    def layer_out(s):
-        total = mid_own[s] + rs_mlp.finish(s) + b_fc2
-        act_ol[slot_rows(s, t), :] = jnp.where(visible_rows(s, t), total, 0.0).astype(bf16)
-        ag_out.start(s)
-
+        if s == 0:
+            go(s_fc2, s_fc1, s_wout)
+        if s == 1:
+            go(s_qa, s_qb)
+    small_copy(0).start()
+    go(s_fc2, s_fc1)
+    small_add(0)
+    go(s_qa, s_qb)
+    small_add(1)
+    ag_in.forward(parts - 1)
+    i = 2
+    while s_qa or s_qb or s_fc2 or s_fc1 or s_wout:
+        go(s_qa, s_qb, s_wout, s_fc2, s_fc1)
+        if i < len(hops):
+            small_add(i)
+            i += 1
+    for j in range(i, len(hops)):
+        small_add(j)
+
+    outs = [
+        fetch(g_fc2, out_fc2),
+        fetch(g_fc1, out_fc1),
+        fetch(g_wout, out_wout),
+        fetch(g_qkv, out_qkv),
+        fetch(small.at[len(hops)], out_small),
+    ]
     for s in range(parts):
-        layer_out(s)
-    ag_in.forward(parts - 1)
-
-    def small_copy(i, rows, target):
-        return remote(
-            sems, small_base + i, small.at[i, pl.ds(0, rows)], small_got.at[i, pl.ds(0, rows)], target
-        )
-
-    hops = [(8, {"tensor": sib}), (8, {"tensor": opp})]
-    for b in range(log_n):
-        step = 1 << b
-        hops.append((16, {"dp": dp + step * (1 - 2 * lax.rem(dp // step, 2))}))
-    for i, (rows, target) in enumerate(hops):
-        cp = small_copy(i, rows, target)
-        cp.start()
-        cp.wait()
-        small[i + 1, 0:rows] = small[i, 0:rows] + small_got[i, 0:rows]
-        if rows < 16:
-            small[i + 1, rows:16] = small[i, rows:16]
-        go(s_qkv)
-        go(s_fc2)
-        go(s_fc1)
-        go(s_wout)
-
-    outs = []
-    for steps, ref, dst in (
-        (s_fc2, g_fc2, out_fc2),
-        (s_fc1, g_fc1, out_fc1),
-        (s_wout, g_wout, out_wout),
-    ):
-        go(steps, len(steps))
-        outs.append(fetch(ref, dst))
-    outs.append(fetch(small.at[len(hops)], out_small))
+        ag_out.finish(s)
+    outs.append(fetch(act_ol, out_layer))
     for s in range(parts):
         ag_in.finish(s)
     outs.append(fetch(n2_oi, out_input))
-    for s in range(parts):
-        ag_out.forward(s)
-    for s in range(parts):
-        ag_out.finish(s)
-    outs.append(fetch(act_ol, out_layer))
-    go(s_qkv, len(s_qkv))
-    outs.append(fetch(g_qkv, out_qkv))
     for cp in outs:
         cp.wait()
 
 
 def sincos_rows(feature_count):
     half_width = feature_count // 6
-    ladder = jnp.arange(half_width, dtype=f32) / half_width
-    frequency = jnp.power(10000.0, -ladder)
-    angles = jnp.arange(COORDS, dtype=jnp.int32).astype(f32)[:, None] * frequency[None, :]
-    return jnp.concatenate([jnp.sin(angles), jnp.cos(angles)], axis=1)
+    ladder = np.arange(half_width, dtype=np.float32) / np.float32(half_width)
+    frequency = np.power(np.float32(10000.0), -ladder).astype(np.float32)
+    angles = (np.arange(COORDS, dtype=np.float32)[:, None] * frequency[None, :]).astype(np.float32)
+    wide = angles.astype(np.float64)
+    left = np.concatenate([np.sin(wide), np.cos(wide)], axis=1)
+    terms = []
+    for _ in range(3):
+        terms.append(left.astype(np.float32).astype(ml_dtypes.bfloat16))
+        left = left - terms[-1].astype(np.float64)
+    return jnp.asarray(np.concatenate(terms, axis=0))
 
 
 def on_device(
@@ -753,14 +782,6 @@
     parts = tokens // (4 * BLK)
     log_n = n_dp.bit_length() - 1
     size = 4 * BLK
-    pad = lambda v: jnp.pad(v, (0, width - v.shape[0]))
-    vecs = jnp.stack(
-        [
-            pad(v.astype(f32))
-            for v in (ln1_gain, ln1_shift, ln2_gain, ln2_shift, b_out, b_fc2, b_fc1, b_qv[0], b_qv[1])
-        ]
-        + [jnp.zeros((width,), f32)] * 7
-    )
     got = Reduce.got_rows
     vmem = lambda *s: pltpu.VMEM(s, bf16)
     vmem32 = lambda *s: pltpu.VMEM(s, f32)
@@ -801,18 +822,18 @@
         vmem(got(ff, 3, log_n), width),
         vmem(got(width, 3, log_n), width),
         vmem(got(hd, 2, log_n), width),
-        vmem(got(width, 3, log_n), 3 * hd),
+        vmem(got(width // 2, 3, log_n), 3 * hd),
+        vmem(got(width // 2, 3, log_n), 3 * hd),
         pltpu.VMEM((tokens, BLK), jnp.int32),
-        vmem(3 * COORDS, 2 * (width // 6)),
         vmem32(3 + log_n, 16, width),
         vmem32(2 + log_n, 16, width),
         vmem32(8, ff),
     ]
-    n_sems = 3 + 4 * 3 * parts + 3 * 2 * parts + 3 * (log_n + 3) + (log_n + 2) + 2 + log_n
+    n_sems = 3 + 4 * 3 * parts + 3 * 2 * parts + 4 * (log_n + 3) + (log_n + 2) + 2 + log_n
     scratch += [
         pltpu.SemaphoreType.DMA((n_sems,)),
         pltpu.SemaphoreType.DMA((n_sems,)),
-        pltpu.SemaphoreType.REGULAR((11,)),
+        pltpu.SemaphoreType.REGULAR((14,)),
         pltpu.SemaphoreType.DMA((4 * parts * 2 + parts + 3 + 7,)),
     ]
     shape = jax.ShapeDtypeStruct
@@ -830,7 +851,7 @@
             shape((width, 3 * hd), bf16),
             shape((16, width), f32),
         ),
-        in_specs=[pl.BlockSpec(memory_space=pltpu.SMEM), hbm, hbm, here, here, hbm, hbm, hbm, here, here],
+        in_specs=[pl.BlockSpec(memory_space=pltpu.SMEM), hbm, hbm, here, here, hbm, hbm, hbm] + [here] * 9,
         out_specs=(hbm,) * 7,
         scratch_shapes=scratch,
         compiler_params=pltpu.CompilerParams(
@@ -841,11 +862,18 @@
         layer_input,
         out_grad,
         patch_coords,
-        w_qkv.reshape(width, 3 * hd),
+        w_qkv.reshape(width, 3 * hd).T,
         w_out,
         w_fc1,
         w_fc2,
-        vecs,
+        ln1_gain,
+        ln1_shift,
+        ln2_gain,
+        ln2_shift,
+        b_out,
+        b_fc2,
+        b_fc1,
+        b_qv,
         sincos_rows(width),
     )
     layer_output, input_grad, g_fc2, g_fc1, g_wout, g_qkv, small = results

time: 218 us -> 192 us (0.88)
  Pallas kernels: 192 us -> 176 us
  local copies, waits for them, and re-layouts: 15.9 us -> 6.85 us
    pallas_call x1, Pallas kernels: 192 us -> 176 us  [on_device(): pl.pallas_call(functools.partial(layer_kernel, (parts, log_n, heads)), na...]
    another operation x13 -> x0, local copies, waits for them, and re-layouts: 6.09 us -> none  [on_device(): jnp.stack([pad(v.astype(f32)) for v in (ln1_gain, ln1_shift, ln2_gain, ln...]
    reshape x1 -> x0, local copies, waits for them, and re-layouts: 2.22 us -> none  [on_device(): w_qkv.reshape(width, 3 * hd)]
where the time goes in v3:
time: 192 us
  Pallas kernels  176 us (92%)
  other arithmetic  8.3 us (4%)
  local copies, waits for them, and re-layouts  6.85 us (4%)
    pallas_call x1, Pallas kernels, on_device(): pl.pallas_call(functools.partial(layer_kernel, (parts, log_n, heads)), na...  176 us
    convert_element_type x1, other arithmetic, on_device(): input_grad.astype(f32)  4.29 us

profile of v3, /device:TPU:0, one launch (start us, length us, event | category | flops | bytes accessed | tf_op | source)
XLA Modules:
  0.0 191.9 jit_solution(3449002050789697568)
XLA Ops:
  0.7 176.0 %layer.1 = (bf16[1536,768]{1,0:T(8,128)(2,1)}, bf16[1536,768]{1,0:T(8,128)(2,1)}, bf16[768,768]{1,0:T(8,128)(2,1)}, bf16[768,768]{1,0:T(8,128)(2,1)}, bf16[192,7...) custom-call(s32[4]{0:T(128)} %lens.1, bf16[1536,768]{1,0:T(8,128)(2,1)} %x_in.1, ...), custom_call_target="tpu_custom_call" | custom-call | tf_op jit(solution)/shard_map/layer/pallas_call | solution.py:842
  176.7 0.0 copy-start.3
  176.7 4.3 %convert_element_type.13 = f32[1536,768]{1,0:T(8,128)} convert(bf16[1536,768]{1,0:T(8,128)(2,1)} %get-tuple-element.22) | non-fusion elementwise | flops 1179648 | bytes 7077888 | tf_op jit(solution)/shard_map/convert_element_type | solution.py:882
  181.0 0.0 copy-start.4
  181.0 0.0 copy-start.2
  181.0 1.6 slice_reduce_fusion
  182.6 0.0 copy-done.3
  182.6 1.5 copy.32
  184.1 0.0 copy-start.1
  184.1 1.4 slice.26
  185.5 0.0 copy-done.4
  185.5 0.9 convert_element_type.14
  186.3 0.0 copy-done.2
  186.4 1.6 convert_element_type.15
  187.9 0.0 copy-start
  187.9 0.0 copy-done.1
  187.9 1.6 convert_element_type.16
  189.5 0.9 copy-done
  190.4 1.4 copy.34
Async XLA Ops:
  176.7 5.9 %copy-start.3 = (bf16[768,576]{1,0:T(8,128)(2,1)S(1)}, bf16[768,576]{1,0:T(8,128)(2,1)}, u32[]{:S(2)}) copy-start(bf16[768,576]{1,0:T(8,128)(2,1)} %get-tuple-element.24) | copy-start | bytes 2654212
  181.0 4.5 %copy-start.4 = (bf16[192,768]{1,0:T(8,128)(2,1)S(1)}, bf16[192,768]{1,0:T(8,128)(2,1)}, u32[]{:S(2)}) copy-start(bf16[192,768]{1,0:T(8,128)(2,1)} %get-tuple-element.25) | copy-start | bytes 884740
  181.0 5.4 %copy-start.2 = (bf16[768,768]{1,0:T(8,128)(2,1)S(1)}, bf16[768,768]{1,0:T(8,128)(2,1)}, u32[]{:S(2)}) copy-start(bf16[768,768]{1,0:T(8,128)(2,1)} %get-tuple-element.26) | copy-start | bytes 3538948
  184.1 3.8 %copy-start.1 = (bf16[768,768]{1,0:T(8,128)(2,1)S(1)}, bf16[768,768]{1,0:T(8,128)(2,1)}, u32[]{:S(2)}) copy-start(bf16[768,768]{1,0:T(8,128)(2,1)} %get-tuple-element.27) | copy-start | bytes 3538948
  187.9 2.5 %copy-start = (bf16[1536,768]{1,0:T(8,128)(2,1)S(1)}, bf16[1536,768]{1,0:T(8,128)(2,1)}, u32[]{:S(2)}) copy-start(bf16[1536,768]{1,0:T(8,128)(2,1)} %get-tuple-element.63) | copy-start | bytes 7077892

commit v4 on v3

--- a/solution.py
+++ b/solution.py
@@ -15,6 +15,13 @@
 LOG2E = 1.4426950408889634
 BLK = 128
 COORDS = 64
+BEFORE_ATTENTION = ["wg2", "f2a", "f2b", "f2c", "n2b", "mla", "f2a", "f2b", "wg1a", "wg1b", "f2c", "wg1c", "f1a", "f1b", "f1c", "f2a", "f2b", "mgf", "md0", "md1", "f2c", "md2", "f2a", "gw", "w"]
+IN_ATTENTION = (
+    [["lo0", "f2b", "f1a"], ["lo1", "f2a", "f2c", "f1b", "w"], ["f2b"]],
+    [["lo2", "f2c", "f1a", "f2a", "f1c", "f1b"], ["of0", "f2b", "w"], ["f2c"]],
+    [["of1", "f1a"], ["f2b"], ["of2", "f2a"]],
+)
+AFTER_ATTENTION = ["st0", "f1c", "wqa", "qa", "f2c", "f1b", "st1", "w", "na0", "wqb", "qb", "wqc", "qc", "f1a", "st2", "na1", "f1c", "sums", "qa", "f1b", "na2", "w", "f1a", "nb0", "f1c", "qa", "qb", "f1b", "nb1", "fo", "qc", "w", "nb2", "sm", "f1c", "f1a", "qa", "sm", "qb", "if0", "qc", "f1b", "qa", "qb", "qc", "if1", "fi0", "qa", "f1c", "qb", "qc", "if2", "fi1", "sm", "qb", "qa", "qc", "sm", "sm", "qb", "qc", "sm"]
 f32 = jnp.float32
 bf16 = jnp.bfloat16
 
@@ -59,6 +66,7 @@
         self.count = 0
         self.ready_count = 0
         self.ready = None
+        self.one = None
         self.send = None
         self.recv = None
 
@@ -158,17 +166,17 @@
 
 
 class Reduce:
-    def __init__(self, sems, ref, got, rows, cols, halvings, order, dp, log_n, first=0):
+    def __init__(self, sems, ref, got, rows, cols, halvings, order, dp, log_n, first=0, spot=0):
         self.sems, self.ref, self.got, self.cols = sems, ref, got, cols
         rest = [b for b in range(log_n) if b not in order[:halvings]]
         self.bits = list(order[:halvings]) + rest
         self.halvings = halvings
-        self.dp = dp
+        self.partners = [dp + (1 << b) * (1 - 2 * lax.rem(dp // (1 << b), 2)) for b in self.bits]
         self.base = sems.take(len(self.bits) + halvings)
         self.ready = sems.ready_count
         sems.ready_count += halvings
         self.low, self.size, self.spot = [first], [rows], []
-        at = 0
+        at = spot
         for j, b in enumerate(self.bits):
             side = lax.rem(dp // (1 << b), 2)
             if j < halvings:
@@ -186,8 +194,7 @@
         return sum(rows >> (j + 1) for j in range(halvings)) + (log_n - halvings) * (rows >> halvings)
 
     def partner(self, j):
-        step = 1 << self.bits[j]
-        return {"dp": self.dp + step * (1 - 2 * lax.rem(self.dp // step, 2))}
+        return {"dp": self.partners[j]}
 
     def at(self, ref, low, size):
         if not isinstance(low, int):
@@ -226,7 +233,7 @@
         if j < self.halvings:
             pl.semaphore_signal(
                 self.sems.ready.at[self.ready + j],
-                inc=1,
+                inc=self.sems.one,
                 device_id=self.partner(j),
                 device_id_type=pl.DeviceIdType.MESH,
             )
@@ -235,7 +242,7 @@
         mine[...] = (mine[...].astype(f32) + theirs[...].astype(f32)).astype(bf16)
 
     def give(self, j):
-        pl.semaphore_wait(self.sems.ready.at[self.ready + j], 1)
+        pl.semaphore_wait(self.sems.ready.at[self.ready + j], self.sems.one)
         self.copy_back(j).start()
 
     def take(self, j):
@@ -326,8 +333,7 @@
     r_fc2,
     r_fc1,
     r_wout,
-    r_qa,
-    r_qb,
+    r_qkv,
     segk,
     small,
     small_got,
@@ -349,6 +355,7 @@
 
     sems = Sems()
     sems.send, sems.recv, sems.ready = send, recv, ready
+    sems.one = lax.rem(t, 1) + 1
 
     def part_rows(s):
         return pl.ds(pl.multiple_of(s * size, size), size)
@@ -367,12 +374,22 @@
     rs_n2 = Scatter(sems, parts, (part0, got_a0, got_b0), t)
     rs_mlp = Scatter(sems, parts, (part1, got_a1, got_b1), t)
     rs_n1 = Scatter(sems, parts, (part0, got_a0, got_b0), t)
-    dp_fc2 = Reduce(sems, g_fc2, r_fc2, width, width, 3, (0, 1, 2), dp, log_n)
-    dp_fc1 = Reduce(sems, g_fc1, r_fc1, width, width, 3, (1, 0, 2), dp, log_n)
-    dp_wout = Reduce(sems, g_wout, r_wout, hd, width, 2, (1, 0), dp, log_n)
-    half = width // 2
-    dp_qa = Reduce(sems, g_qkv, r_qa, half, 3 * hd, 3, (0, 1, 2), dp, log_n)
-    dp_qb = Reduce(sems, g_qkv, r_qb, half, 3 * hd, 3, (1, 0, 2), dp, log_n, half)
+    third = width // 3
+    along_x, along_z = (0, 1, 2), (1, 0, 2)
+    chains = {}
+
+    def unit(name, ref, got, out, rows, cols, halvings, order, i=0):
+        first, spot = i * rows, i * Reduce.got_rows(rows, halvings, log_n)
+        total = Reduce(sems, ref, got, rows, cols, halvings, order, dp, log_n, first, spot)
+        chains[name] = (total.steps(), ref, out, pl.ds(first, rows))
+
+    for i in range(3):
+        unit("f2" + "abc"[i], g_fc2, r_fc2, out_fc2, third, width, 3, along_x if i else along_z, i)
+    for i in range(3):
+        unit("f1" + "abc"[i], g_fc1, r_fc1, out_fc1, third, width, 3, along_x, i)
+    unit("w", g_wout, r_wout, out_wout, hd, width, 2, along_z[:2])
+    for i in range(3):
+        unit("q" + "abc"[i], g_qkv, r_qkv, out_qkv, third, 3 * hd, 3, along_x, i)
     small_base = sems.take(2 + log_n)
 
     n_local = [0]
@@ -466,6 +483,7 @@
         return carry
 
     lax.fori_loop(0, parts, project, 0)
+    ag_w.forward(0)
 
     def attend(s, carry):
         place = jnp.concatenate(
@@ -496,7 +514,6 @@
         return carry
 
     lax.fori_loop(0, parts, attend, 0)
-    ag_w.forward(0)
     for cp in tg_loads:
         cp.wait()
     fc1_load.wait()
@@ -522,10 +539,6 @@
         ag_mg.start(s)
 
     def feed(s, carry):
-        @pl.when(s == parts - 1)
-        def _():
-            ag_mix.forward(s)
-
         ag_mix.finish(s)
         attn = mm_tn(mix[s], w_out[...])
         middle = hidden_of(s) + attn + b_out
@@ -555,62 +568,157 @@
         def _():
             ag_mg.forward(s - 2)
 
+        @pl.when(s == parts - 2)
+        def _():
+            ag_mix.forward(parts - 1)
+
         rs_mlp.store(s, mm(act_ol[part_rows(s), :], w_fc2[...]))
         rs_n2.across(s)
         return carry
 
     lax.fori_loop(0, parts, feed, 0)
 
-    def weight_grad(dst, left, right, cols, first=0, last=None):
-        last = left.shape[1] if last is None else last
-        for i in range(first, last, 256 if (last - first) % 256 == 0 else last - first):
-            n = 256 if (last - first) % 256 == 0 else last - first
-            dst[i : i + n, :cols] = mm_tn(left[:, i : i + n], right[:, :cols]).astype(bf16)
-
-    s_fc2, s_fc1, s_wout = dp_fc2.steps(), dp_fc1.steps(), dp_wout.steps()
-    s_qa, s_qb = dp_qa.steps(), dp_qb.steps()
-
-    def go(*chains):
-        for steps in chains:
-            if steps:
-                steps.pop(0)()
-
-    weight_grad(g_fc2, act_ol, tg, width)
-    go(s_fc2)
-    for s in range(parts):
-        rs_mlp.start(s)
-    second_norm_back(parts - 1)
-    x_own_loads = [fetch(x_in.at[slot_rows(s, t)], tg.at[own_rows(s, t)]) for s in range(parts)]
-    if parts >= 2:
-        ag_mg.forward(parts - 2)
-    for s in range(parts):
-        rs_mlp.across(s)
-    weight_grad(g_fc1, n2_oi, pg_dq, width)
-    go(s_fc1)
-    ag_mg.forward(parts - 1)
-    for s in range(parts):
-        ag_mg.finish(s)
+    def weight_grad(dst, left, right, cols, first, last):
+        for i in range(first, last):
+            rows = slice(i * third, (i + 1) * third)
+            dst[rows, :cols] = mm_tn(left[:, rows], right[:, :cols]).astype(bf16)
+
+    own = pl.ds(pl.multiple_of(t * hd, hd), hd)
+    outs, ended, x_own_loads = [], [], []
 
     def layer_out(s):
         total = mid_own[s] + rs_mlp.finish(s) + b_fc2
         act_ol[slot_rows(s, t), :] = jnp.where(visible_rows(s, t), total, 0.0).astype(bf16)
         ag_out.start(s)
 
-    for s in range(parts):
+    def mixed_grad(s):
+        ag_mg.finish(s)
         rows = part_rows(s)
-        own = pl.ds(pl.multiple_of(t * hd, hd), hd)
         low = mm_nt(x_mg[rows, :], w_out[own, :]).astype(bf16).astype(f32).T
         for h in range(heads):
             scaled = (low[h * HEAD_DIM : (h + 1) * HEAD_DIM] * linv[h, :, rows]).astype(bf16)
             do_t[h, :, rows] = scaled
             mixed = mix[s, pl.ds(pl.multiple_of(t * hd + h * HEAD_DIM, HEAD_DIM), HEAD_DIM), :]
             delta[h, :, rows] = jnp.sum(scaled.astype(f32) * mixed.astype(f32), axis=0, keepdims=True)
-    own = pl.ds(pl.multiple_of(t * hd, hd), hd)
-    grad_out = mm(mix[0, own, :], x_mg[part_rows(0), :])
-    for s in range(1, parts):
-        grad_out = grad_out + mm(mix[s, own, :], x_mg[part_rows(s), :])
-    g_wout[...] = grad_out.astype(bf16)
-    go(s_wout)
+
+    def out_weight_grad():
+        total = mm(mix[0, own, :], x_mg[part_rows(0), :])
+        for s in range(1, parts):
+            total = total + mm(mix[s, own, :], x_mg[part_rows(s), :])
+        g_wout[...] = total.astype(bf16)
+
+    def first_norm_back(s):
+        if s == 0:
+            for cp in x_own_loads:
+                cp.wait()
+        u = rs_n1.finish(s)
+        hidden = tg[own_rows(s, t), :].astype(f32) + positions(None, coords[:, slot_rows(s, t)])
+        x_hat, r = norm_parts(hidden)
+        grad = mg_own[s] + norm_back(u, ln1_gain, x_hat, r)
+        small[0, 0:1, :] += jnp.sum(u * x_hat, axis=0, keepdims=True)
+        small[0, 1:2, :] += jnp.sum(u, axis=0, keepdims=True)
+        n2_oi[slot_rows(s, t), :] = grad.astype(bf16)
+        ag_in.start(s)
+
+    def sums():
+        total = jnp.sum(pg_dq[:, : 3 * hd].astype(f32), axis=0, keepdims=True)
+        small[0, 8:9, :] = fc1_sums[0:1, :]
+        small[0, 9:10, :hd] = total[:, :hd]
+        small[0, 10:11, :hd] = total[:, 2 * hd :]
+
+    hops = [(8, {"tensor": sib}), (8, {"tensor": opp})]
+    for b in range(log_n):
+        step = 1 << b
+        hops.append((16, {"dp": dp + step * (1 - 2 * lax.rem(dp // step, 2))}))
+
+    def small_copy(i):
+        rows, target = hops[i]
+        return remote(
+            sems, small_base + i, small.at[i, pl.ds(0, rows)], small_got.at[i, pl.ds(0, rows)], target
+        )
+
+    def small_add(i):
+        rows = hops[i][0]
+        small_copy(i).wait()
+        small[i + 1, 0:rows] = small[i, 0:rows] + small_got[i, 0:rows]
+        if rows < 16:
+            small[i + 1, rows:16] = small[i, rows:16]
+        if i + 1 < len(hops):
+            small_copy(i + 1).start()
+
+    small_steps = [lambda: small_copy(0).start()] + [
+        functools.partial(small_add, i) for i in range(len(hops))
+    ]
+
+    def input_out(s):
+        ag_in.finish(s)
+        for o in range(4):
+            outs.append(fetch(n2_oi.at[slot_rows(s, o)], out_input.at[slot_rows(s, o)]))
+
+    def do(token):
+        kind, at = token[:2], token[2:]
+        if token in chains:
+            steps, ref, out, rows = chains[token]
+            steps.pop(0)()
+            if not steps:
+                ended.append((ref, out, rows))
+        elif token == "wg2":
+            weight_grad(g_fc2, act_ol, tg, width, 0, 3)
+            for s in range(parts):
+                rs_mlp.start(s)
+        elif token == "n2b":
+            second_norm_back(parts - 1)
+            for s in range(parts):
+                x_own_loads.append(fetch(x_in.at[slot_rows(s, t)], tg.at[own_rows(s, t)]))
+            ag_mg.forward(parts - 2)
+        elif token == "mla":
+            for s in range(parts):
+                rs_mlp.across(s)
+        elif kind == "wg":
+            i = "abc".index(token[3])
+            weight_grad(g_fc1, n2_oi, pg_dq, width, i, i + 1)
+        elif token == "mgf":
+            ag_mg.forward(parts - 1)
+        elif kind == "md":
+            mixed_grad(int(at))
+        elif token == "gw":
+            out_weight_grad()
+        elif kind == "lo":
+            layer_out(int(at))
+        elif kind == "of":
+            ag_out.forward(int(at))
+        elif kind == "st":
+            s = int(at)
+            rs_n1.store(s, mm(pg_dq[part_rows(s), : 3 * hd], w_qkv[...]))
+            rs_n1.start(s)
+        elif kind == "na":
+            rs_n1.across(int(at))
+        elif kind == "wq":
+            i = "abc".index(at)
+            weight_grad(g_qkv, n1, pg_dq, 3 * hd, i, i + 1)
+        elif kind == "nb":
+            first_norm_back(int(at))
+        elif kind == "if":
+            ag_in.forward(int(at))
+        elif kind == "fi":
+            input_out(int(at))
+        elif token == "sums":
+            sums()
+        elif token == "sm":
+            small_steps.pop(0)()
+        elif token == "fo":
+            for s in range(parts):
+                ag_out.finish(s)
+            outs.append(fetch(act_ol, out_layer))
+
+    def run(tokens, in_loop=False):
+        for token in tokens:
+            do(token)
+            while ended and not in_loop:
+                ref, out, rows = ended.pop(0)
+                outs.append(fetch(ref.at[rows], out.at[rows]))
+
+    run(BEFORE_ATTENTION)
 
     for h in range(heads):
         rows3[0] = v_t[h].astype(f32).T.astype(bf16)
@@ -636,108 +744,27 @@
             def _():
                 acc[...] += dq
 
+            for k in range(2):
+
+                @pl.when(s == k)
+                def _(k=k):
+                    run(IN_ATTENTION[h][k], True)
+
             return carry
 
         lax.fori_loop(0, parts, back, 0)
         pg_dq[:, h * HEAD_DIM : (h + 1) * HEAD_DIM] = (acc[...].T * (1.0 / HEAD_DIM**0.5)).astype(bf16)
-        go(s_fc2, s_fc1)
-        if h == 0:
-            layer_out(0)
-        if h == 1:
-            go(s_wout)
-            for s in range(1, parts):
-                layer_out(s)
-        if h == heads - 1:
-            go(s_wout)
-            for s in range(parts):
-                ag_out.forward(s)
-
-    for s in range(parts):
-        rs_n1.store(s, mm(pg_dq[part_rows(s), : 3 * hd], w_qkv[...]))
-        rs_n1.start(s)
-        if s >= 1:
-            rs_n1.across(s - 1)
-        if s == 0:
-            weight_grad(g_qkv, n1, pg_dq, 3 * hd, 0, half)
-            go(s_qa)
-        if s == 1:
-            weight_grad(g_qkv, n1, pg_dq, 3 * hd, half, width)
-            go(s_qb)
-    rs_n1.across(parts - 1)
-    go(s_fc2, s_fc1, s_wout)
-    sums = jnp.sum(pg_dq[:, : 3 * hd].astype(f32), axis=0, keepdims=True)
-    small[0, 8:9, :] = fc1_sums[0:1, :]
-    small[0, 9:10, :hd] = sums[:, :hd]
-    small[0, 10:11, :hd] = sums[:, 2 * hd :]
-
-    def first_norm_back(s):
-        u = rs_n1.finish(s)
-        hidden = tg[own_rows(s, t), :].astype(f32) + positions(None, coords[:, slot_rows(s, t)])
-        x_hat, r = norm_parts(hidden)
-        grad = mg_own[s] + norm_back(u, ln1_gain, x_hat, r)
-        small[0, 0:1, :] += jnp.sum(u * x_hat, axis=0, keepdims=True)
-        small[0, 1:2, :] += jnp.sum(u, axis=0, keepdims=True)
-        n2_oi[slot_rows(s, t), :] = grad.astype(bf16)
-        ag_in.start(s)
-
-    hops = [(8, {"tensor": sib}), (8, {"tensor": opp})]
-    for b in range(log_n):
-        step = 1 << b
-        hops.append((16, {"dp": dp + step * (1 - 2 * lax.rem(dp // step, 2))}))
-
-    def small_copy(i):
-        rows, target = hops[i]
-        return remote(
-            sems, small_base + i, small.at[i, pl.ds(0, rows)], small_got.at[i, pl.ds(0, rows)], target
-        )
-
-    def small_add(i):
-        rows = hops[i][0]
-        small_copy(i).wait()
-        small[i + 1, 0:rows] = small[i, 0:rows] + small_got[i, 0:rows]
-        if rows < 16:
-            small[i + 1, rows:16] = small[i, rows:16]
-        if i + 1 < len(hops):
-            small_copy(i + 1).start()
-
-    for cp in x_own_loads:
-        cp.wait()
-    for s in range(parts):
-        first_norm_back(s)
-        if s >= 1:
-            ag_in.forward(s - 1)
-        if s == 0:
-            go(s_fc2, s_fc1, s_wout)
-        if s == 1:
-            go(s_qa, s_qb)
-    small_copy(0).start()
-    go(s_fc2, s_fc1)
-    small_add(0)
-    go(s_qa, s_qb)
-    small_add(1)
-    ag_in.forward(parts - 1)
-    i = 2
-    while s_qa or s_qb or s_fc2 or s_fc1 or s_wout:
-        go(s_qa, s_qb, s_wout, s_fc2, s_fc1)
-        if i < len(hops):
-            small_add(i)
-            i += 1
-    for j in range(i, len(hops)):
-        small_add(j)
-
-    outs = [
-        fetch(g_fc2, out_fc2),
-        fetch(g_fc1, out_fc1),
-        fetch(g_wout, out_wout),
-        fetch(g_qkv, out_qkv),
-        fetch(small.at[len(hops)], out_small),
-    ]
-    for s in range(parts):
-        ag_out.finish(s)
-    outs.append(fetch(act_ol, out_layer))
-    for s in range(parts):
-        ag_in.finish(s)
-    outs.append(fetch(n2_oi, out_input))
+        run(IN_ATTENTION[h][2])
+
+    run(AFTER_ATTENTION)
+    while small_steps or any(chain[0] for chain in chains.values()):
+        for name in ("qa", "qb", "qc", "f2a", "f2b", "f2c", "f1a", "f1b", "f1c", "w"):
+            if chains[name][0]:
+                run([name])
+        if small_steps:
+            do("sm")
+    outs.append(fetch(small.at[len(hops)], out_small))
+    input_out(parts - 1)
     for cp in outs:
         cp.wait()
 
@@ -819,22 +846,21 @@
         vmem(width, ff),
         vmem(hd, width),
         vmem(width, 3 * hd),
-        vmem(got(ff, 3, log_n), width),
-        vmem(got(width, 3, log_n), width),
+        vmem(3 * got(width // 3, 3, log_n), width),
+        vmem(3 * got(width // 3, 3, log_n), width),
         vmem(got(hd, 2, log_n), width),
-        vmem(got(width // 2, 3, log_n), 3 * hd),
-        vmem(got(width // 2, 3, log_n), 3 * hd),
+        vmem(3 * got(width // 3, 3, log_n), 3 * hd),
         pltpu.VMEM((tokens, BLK), jnp.int32),
         vmem32(3 + log_n, 16, width),
         vmem32(2 + log_n, 16, width),
         vmem32(8, ff),
     ]
-    n_sems = 3 + 4 * 3 * parts + 3 * 2 * parts + 4 * (log_n + 3) + (log_n + 2) + 2 + log_n
+    n_sems = 3 + 4 * 3 * parts + 3 * 2 * parts + 9 * (log_n + 3) + (log_n + 2) + 2 + log_n
     scratch += [
         pltpu.SemaphoreType.DMA((n_sems,)),
         pltpu.SemaphoreType.DMA((n_sems,)),
-        pltpu.SemaphoreType.REGULAR((14,)),
-        pltpu.SemaphoreType.DMA((4 * parts * 2 + parts + 3 + 7,)),
+        pltpu.SemaphoreType.REGULAR((29,)),
+        pltpu.SemaphoreType.DMA((4 * parts * 2 + parts + 3 + 10 + 2 + 4 * parts,)),
     ]
     shape = jax.ShapeDtypeStruct
     hbm = pl.BlockSpec(memory_space=pl.ANY)

time: 192 us -> 168 us (0.88)
  Pallas kernels: 176 us -> 152 us
    pallas_call x1, Pallas kernels: 176 us -> 152 us  [on_device(): pl.pallas_call(functools.partial(layer_kernel, (parts, log_n, heads)), na...]
where the time goes in v4:
time: 168 us; the launch traced here: 167 us
  Pallas kernels  152 us (90%)
  other arithmetic  8.3 us (5%)
  local copies, waits for them, and re-layouts  6.85 us (4%)
    pallas_call x1, Pallas kernels, on_device(): pl.pallas_call(functools.partial(layer_kernel, (parts, log_n, heads)), na...  152 us
    convert_element_type x1, other arithmetic, on_device(): input_grad.astype(f32)  4.29 us

profile of v4, /device:TPU:0, one launch (start us, length us, event | category | flops | bytes accessed | tf_op | source)
XLA Modules:
  0.0 167.5 jit_solution(6367820067259626672)
XLA Ops:
  0.7 151.7 %layer.1 = (bf16[1536,768]{1,0:T(8,128)(2,1)}, bf16[1536,768]{1,0:T(8,128)(2,1)}, bf16[768,768]{1,0:T(8,128)(2,1)}, bf16[768,768]{1,0:T(8,128)(2,1)}, bf16[192,7...) custom-call(s32[4]{0:T(128)} %lens.1, bf16[1536,768]{1,0:T(8,128)(2,1)} %x_in.1, ...), custom_call_target="tpu_custom_call" | custom-call | tf_op jit(solution)/shard_map/layer/pallas_call | solution.py:868
  152.3 0.0 copy-start.3
  152.3 4.3 %convert_element_type.13 = f32[1536,768]{1,0:T(8,128)} convert(bf16[1536,768]{1,0:T(8,128)(2,1)} %get-tuple-element.22) | non-fusion elementwise | flops 1179648 | bytes 7077888 | tf_op jit(solution)/shard_map/convert_element_type | solution.py:908
  156.6 0.0 copy-start.4
  156.6 0.0 copy-start.2
  156.6 1.6 slice_reduce_fusion
  158.3 0.0 copy-done.3
  158.3 1.5 copy.32
  159.8 0.0 copy-start.1
  159.8 1.4 slice.26
  161.1 0.0 copy-done.4
  161.1 0.9 convert_element_type.14
  162.0 0.0 copy-done.2
  162.0 1.6 convert_element_type.15
  163.6 0.0 copy-start
  163.6 0.0 copy-done.1
  163.6 1.6 convert_element_type.16
  165.1 0.9 copy-done
  166.1 1.4 copy.34
Async XLA Ops:
  152.3 5.9 %copy-start.3 = (bf16[768,576]{1,0:T(8,128)(2,1)S(1)}, bf16[768,576]{1,0:T(8,128)(2,1)}, u32[]{:S(2)}) copy-start(bf16[768,576]{1,0:T(8,128)(2,1)} %get-tuple-element.24) | copy-start | bytes 2654212
  156.6 4.5 %copy-start.4 = (bf16[192,768]{1,0:T(8,128)(2,1)S(1)}, bf16[192,768]{1,0:T(8,128)(2,1)}, u32[]{:S(2)}) copy-start(bf16[192,768]{1,0:T(8,128)(2,1)} %get-tuple-element.25) | copy-start | bytes 884740
  156.6 5.4 %copy-start.2 = (bf16[768,768]{1,0:T(8,128)(2,1)S(1)}, bf16[768,768]{1,0:T(8,128)(2,1)}, u32[]{:S(2)}) copy-start(bf16[768,768]{1,0:T(8,128)(2,1)} %get-tuple-element.26) | copy-start | bytes 3538948
  159.8 3.8 %copy-start.1 = (bf16[768,768]{1,0:T(8,128)(2,1)S(1)}, bf16[768,768]{1,0:T(8,128)(2,1)}, u32[]{:S(2)}) copy-start(bf16[768,768]{1,0:T(8,128)(2,1)} %get-tuple-element.27) | copy-start | bytes 3538948
  163.6 2.5 %copy-start = (bf16[1536,768]{1,0:T(8,128)(2,1)S(1)}, bf16[1536,768]{1,0:T(8,128)(2,1)}, u32[]{:S(2)}) copy-start(bf16[1536,768]{1,0:T(8,128)(2,1)} %get-tuple-element.63) | copy-start | bytes 7077892

commit v5 on v4

--- a/solution.py
+++ b/solution.py
@@ -15,13 +15,13 @@
 LOG2E = 1.4426950408889634
 BLK = 128
 COORDS = 64
-BEFORE_ATTENTION = ["wg2", "f2a", "f2b", "f2c", "n2b", "mla", "f2a", "f2b", "wg1a", "wg1b", "f2c", "wg1c", "f1a", "f1b", "f1c", "f2a", "f2b", "mgf", "md0", "md1", "f2c", "md2", "f2a", "gw", "w"]
+BEFORE_ATTENTION = ["wg2", "f2a", "f2b", "f2c", "mp", "wg1a", "f1a", "mf1", "wg1b", "f1b", "wg1c", "f1c", "vr", "f2a", "f2b", "n2b", "mla", "md0"]
 IN_ATTENTION = (
-    [["lo0", "f2b", "f1a"], ["lo1", "f2a", "f2c", "f1b", "w"], ["f2b"]],
-    [["lo2", "f2c", "f1a", "f2a", "f1c", "f1b"], ["of0", "f2b", "w"], ["f2c"]],
-    [["of1", "f1a"], ["f2b"], ["of2", "f2a"]],
+    [["f2c", "f2a"], [], ["mf2", "f2c", "f1a", "md1", "f2a"]],
+    [["lo0", "f1b", "f2c"], ["f2a", "f1a"], ["lo1", "f1b", "f2c", "f2b", "f1c", "md2", "gw", "w", "lo2", "f2a"]],
+    [["f1a", "f1b"], ["of0", "f2c"], ["f2b", "w", "f1c"]],
 )
-AFTER_ATTENTION = ["st0", "f1c", "wqa", "qa", "f2c", "f1b", "st1", "w", "na0", "wqb", "qb", "wqc", "qc", "f1a", "st2", "na1", "f1c", "sums", "qa", "f1b", "na2", "w", "f1a", "nb0", "f1c", "qa", "qb", "f1b", "nb1", "fo", "qc", "w", "nb2", "sm", "f1c", "f1a", "qa", "sm", "qb", "if0", "qc", "f1b", "qa", "qb", "qc", "if1", "fi0", "qa", "f1c", "qb", "qc", "if2", "fi1", "sm", "qb", "qa", "qc", "sm", "sm", "qb", "qc", "sm"]
+AFTER_ATTENTION = ["fz", "of1", "f1a", "st0", "f2a", "f1b", "wqa", "qa", "st1", "f2b", "w", "na0", "of2", "wqb", "qb", "wqc", "qc", "f2c", "f1c", "st2", "na1", "f1a", "sums", "qa", "f1b", "na2", "f2b", "w", "nb0", "qb", "qc", "f1c", "nb1", "fo", "qa", "f1a", "nb2", "sm", "f2b", "sm", "f1b", "w", "if0", "qc", "qb", "f1c", "qa", "if1", "fi0", "w", "qc", "qb", "qa", "if2", "fi1", "f1c", "sm", "qc", "qb", "qa", "sm", "qc", "qb", "sm", "qa", "qc", "qb", "sm"]
 f32 = jnp.float32
 bf16 = jnp.bfloat16
 
@@ -292,12 +292,12 @@
     v6,
     b_qv,
     tab3,
-    out_layer,
-    out_input,
-    out_fc2,
-    out_fc1,
-    out_wout,
-    out_qkv,
+    act_ol,
+    n2_oi,
+    g_fc2,
+    g_fc1,
+    g_wout,
+    g_qkv,
     out_small,
     x_mg,
     tg,
@@ -313,8 +313,6 @@
     w_fc1,
     w_fc2,
     mid_own,
-    n2_oi,
-    act_ol,
     pg_dq,
     part0,
     got_a0,
@@ -323,13 +321,8 @@
     got_a1,
     got_b1,
     mg_own,
-    do_t,
     delta,
     acc,
-    g_fc2,
-    g_fc1,
-    g_wout,
-    g_qkv,
     r_fc2,
     r_fc1,
     r_wout,
@@ -344,6 +337,7 @@
     local,
 ):
     parts, log_n, heads = geo
+    do_t = v_t
     vecs = (v0, v1, v2, v3, v4, v5, v6)
     size = 4 * BLK
     dp = lax.axis_index("dp")
@@ -378,18 +372,18 @@
     along_x, along_z = (0, 1, 2), (1, 0, 2)
     chains = {}
 
-    def unit(name, ref, got, out, rows, cols, halvings, order, i=0):
+    def unit(name, ref, got, rows, cols, halvings, order, i=0):
         first, spot = i * rows, i * Reduce.got_rows(rows, halvings, log_n)
         total = Reduce(sems, ref, got, rows, cols, halvings, order, dp, log_n, first, spot)
-        chains[name] = (total.steps(), ref, out, pl.ds(first, rows))
+        chains[name] = total.steps()
 
     for i in range(3):
-        unit("f2" + "abc"[i], g_fc2, r_fc2, out_fc2, third, width, 3, along_x if i else along_z, i)
+        unit("f2" + "abc"[i], g_fc2, r_fc2, third, width, 3, along_z if i == 1 else along_x, i)
     for i in range(3):
-        unit("f1" + "abc"[i], g_fc1, r_fc1, out_fc1, third, width, 3, along_x, i)
-    unit("w", g_wout, r_wout, out_wout, hd, width, 2, along_z[:2])
+        unit("f1" + "abc"[i], g_fc1, r_fc1, third, width, 3, along_x, i)
+    unit("w", g_wout, r_wout, hd, width, 2, along_x[:2])
     for i in range(3):
-        unit("q" + "abc"[i], g_qkv, r_qkv, out_qkv, third, 3 * hd, 3, along_x, i)
+        unit("q" + "abc"[i], g_qkv, r_qkv, third, 3 * hd, 3, along_z if i == 2 else along_x, i)
     small_base = sems.take(2 + log_n)
 
     n_local = [0]
@@ -422,10 +416,7 @@
         pl.semaphore_signal(
             barrier, inc=1, device_id={"dp": other}, device_id_type=pl.DeviceIdType.MESH
         )
-    pl.semaphore_wait(barrier, 2 + log_n)
-
-    w_out_load.wait()
-    ag_w.start(0)
+
 
     def row(ref):
         return ref[...].astype(f32).reshape(1, ref.shape[0])
@@ -480,10 +471,16 @@
             k_t[h, :, part_rows(s)] = k[head]
             v_t[h, :, part_rows(s)] = v[head]
             rows3[h, part_rows(s), :] = k[head].astype(f32).T.astype(bf16)
+
+        @pl.when(s == 0)
+        def _():
+            pl.semaphore_wait(barrier, 2 + log_n)
+            ag_w.start(0)
+
         return carry
 
+    w_out_load.wait()
     lax.fori_loop(0, parts, project, 0)
-    ag_w.forward(0)
 
     def attend(s, carry):
         place = jnp.concatenate(
@@ -495,6 +492,12 @@
         )
         allowed = segk[...][:, :1] == segment_of(place)
         for h in range(heads):
+            if h == heads - 1:
+
+                @pl.when(s >= 2)
+                def _():
+                    ag_mix.forward(s - 2)
+
             scores = mm(rows3[h], q_t[h, :, part_rows(s)])
             scores = jnp.where(allowed, scores * (LOG2E / HEAD_DIM**0.5), MASK_FILL)
             top = jnp.max(scores, axis=0, keepdims=True)
@@ -507,9 +510,9 @@
             mix[s, pl.ds(pl.multiple_of(t * hd + h * HEAD_DIM, HEAD_DIM), HEAD_DIM), :] = mixed.astype(bf16)
         ag_mix.start(s)
 
-        @pl.when(s >= 1)
+        @pl.when(s == 1)
         def _():
-            ag_mix.forward(s - 1)
+            ag_w.forward(0)
 
         return carry
 
@@ -557,6 +560,10 @@
         pre = (mm_nt(top, w_fc2[...]) * slope).astype(bf16)
         pg_dq[part_rows(s), :] = pre
         fc1_sums[0:1, :] += jnp.sum(pre.astype(f32), axis=0, keepdims=True)
+        @pl.when(s + 1 < parts)
+        def _():
+            ag_mix.forward(s + 1)
+
         rs_n2.store(s, mm_nt(pre, w_fc1[...]))
         rs_n2.start(s)
 
@@ -568,11 +575,6 @@
         def _():
             ag_mg.forward(s - 2)
 
-        @pl.when(s == parts - 2)
-        def _():
-            ag_mix.forward(parts - 1)
-
-        rs_mlp.store(s, mm(act_ol[part_rows(s), :], w_fc2[...]))
         rs_n2.across(s)
         return carry
 
@@ -584,7 +586,7 @@
             dst[rows, :cols] = mm_tn(left[:, rows], right[:, :cols]).astype(bf16)
 
     own = pl.ds(pl.multiple_of(t * hd, hd), hd)
-    outs, ended, x_own_loads = [], [], []
+    x_own_loads = []
 
     def layer_out(s):
         total = mid_own[s] + rs_mlp.finish(s) + b_fc2
@@ -600,6 +602,15 @@
             do_t[h, :, rows] = scaled
             mixed = mix[s, pl.ds(pl.multiple_of(t * hd + h * HEAD_DIM, HEAD_DIM), HEAD_DIM), :]
             delta[h, :, rows] = jnp.sum(scaled.astype(f32) * mixed.astype(f32), axis=0, keepdims=True)
+
+    def collect(s):
+        rows = part_rows(s)
+        for h in range(heads):
+            low = do_t[h, :, rows].astype(f32).T.astype(bf16)
+            pg_dq[rows, h * HEAD_DIM : (h + 1) * HEAD_DIM] = low
+            key = acc[h, rows, HEAD_DIM:] * (1.0 / HEAD_DIM**0.5)
+            pg_dq[rows, hd + h * HEAD_DIM : hd + (h + 1) * HEAD_DIM] = key.astype(bf16)
+            pg_dq[rows, 2 * hd + h * HEAD_DIM : 2 * hd + (h + 1) * HEAD_DIM] = acc[h, rows, :HEAD_DIM].astype(bf16)
 
     def out_weight_grad():
         total = mm(mix[0, own, :], x_mg[part_rows(0), :])
@@ -650,35 +661,35 @@
         functools.partial(small_add, i) for i in range(len(hops))
     ]
 
-    def input_out(s):
-        ag_in.finish(s)
-        for o in range(4):
-            outs.append(fetch(n2_oi.at[slot_rows(s, o)], out_input.at[slot_rows(s, o)]))
-
     def do(token):
         kind, at = token[:2], token[2:]
         if token in chains:
-            steps, ref, out, rows = chains[token]
-            steps.pop(0)()
-            if not steps:
-                ended.append((ref, out, rows))
+            chains[token].pop(0)()
         elif token == "wg2":
             weight_grad(g_fc2, act_ol, tg, width, 0, 3)
-            for s in range(parts):
+        elif token == "mp":
+
+            def product(s, carry):
+                rs_mlp.store(s, mm(act_ol[part_rows(s), :], w_fc2[...]))
                 rs_mlp.start(s)
+                return carry
+
+            lax.fori_loop(0, parts, product, 0)
+        elif token == "vr":
+            for h in range(heads):
+                rows3[h] = v_t[h].astype(f32).T.astype(bf16)
         elif token == "n2b":
             second_norm_back(parts - 1)
             for s in range(parts):
                 x_own_loads.append(fetch(x_in.at[slot_rows(s, t)], tg.at[own_rows(s, t)]))
-            ag_mg.forward(parts - 2)
         elif token == "mla":
             for s in range(parts):
                 rs_mlp.across(s)
         elif kind == "wg":
             i = "abc".index(token[3])
             weight_grad(g_fc1, n2_oi, pg_dq, width, i, i + 1)
-        elif token == "mgf":
-            ag_mg.forward(parts - 1)
+        elif kind == "mf":
+            ag_mg.forward(int(at))
         elif kind == "md":
             mixed_grad(int(at))
         elif token == "gw":
@@ -687,6 +698,9 @@
             layer_out(int(at))
         elif kind == "of":
             ag_out.forward(int(at))
+        elif token == "fz":
+            for s in range(parts):
+                collect(s)
         elif kind == "st":
             s = int(at)
             rs_n1.store(s, mm(pg_dq[part_rows(s), : 3 * hd], w_qkv[...]))
@@ -701,7 +715,7 @@
         elif kind == "if":
             ag_in.forward(int(at))
         elif kind == "fi":
-            input_out(int(at))
+            ag_in.finish(int(at))
         elif token == "sums":
             sums()
         elif token == "sm":
@@ -709,64 +723,51 @@
         elif token == "fo":
             for s in range(parts):
                 ag_out.finish(s)
-            outs.append(fetch(act_ol, out_layer))
-
-    def run(tokens, in_loop=False):
+
+    def run(tokens):
         for token in tokens:
             do(token)
-            while ended and not in_loop:
-                ref, out, rows = ended.pop(0)
-                outs.append(fetch(ref.at[rows], out.at[rows]))
 
     run(BEFORE_ATTENTION)
 
-    for h in range(heads):
-        rows3[0] = v_t[h].astype(f32).T.astype(bf16)
-        rows3[1] = q_t[h].astype(f32).T.astype(bf16)
-        rows3[2] = do_t[h].astype(f32).T.astype(bf16)
-
-        def back(s, carry, h=h):
-            rows = part_rows(s)
-            p = probs[h, rows, :]
-            wg = mm(rows3[0, rows, :], do_t[h])
-            sg = (p.astype(f32) * (wg - delta[h])).astype(bf16)
-            dv = mm(p, rows3[2])
-            dk = mm(sg, rows3[1]) * (1.0 / HEAD_DIM**0.5)
-            pg_dq[rows, hd + h * HEAD_DIM : hd + (h + 1) * HEAD_DIM] = dk.astype(bf16)
-            pg_dq[rows, 2 * hd + h * HEAD_DIM : 2 * hd + (h + 1) * HEAD_DIM] = dv.astype(bf16)
-            dq = mm(k_t[h, :, rows], sg)
-
-            @pl.when(s == 0)
-            def _():
-                acc[...] = dq
-
-            @pl.when(s > 0)
-            def _():
-                acc[...] += dq
-
-            for k in range(2):
-
-                @pl.when(s == k)
+    for s in range(parts):
+        rows = part_rows(s)
+
+        def back(h, carry, s=s, rows=rows):
+            p = probs[h, :, rows]
+            low = do_t[h, :, rows]
+            wg = mm(rows3[h], low)
+            sg = (p.astype(f32) * (wg - delta[h, :, rows])).astype(bf16)
+            dv = mm(p, low.astype(f32).T.astype(bf16))
+            dk = mm(sg, q_t[h, :, rows].astype(f32).T.astype(bf16))
+            do_t[h, :, rows] = (mm(k_t[h], sg) * (1.0 / HEAD_DIM**0.5)).astype(bf16)
+            if s == 0:
+                acc[h, :, :HEAD_DIM] = dv
+                acc[h, :, HEAD_DIM:] = dk
+            else:
+                acc[h, :, :HEAD_DIM] += dv
+                acc[h, :, HEAD_DIM:] += dk
+            for k in range(heads - 1):
+
+                @pl.when(h == k)
                 def _(k=k):
-                    run(IN_ATTENTION[h][k], True)
+                    run(IN_ATTENTION[s][k])
 
             return carry
 
-        lax.fori_loop(0, parts, back, 0)
-        pg_dq[:, h * HEAD_DIM : (h + 1) * HEAD_DIM] = (acc[...].T * (1.0 / HEAD_DIM**0.5)).astype(bf16)
-        run(IN_ATTENTION[h][2])
+        lax.fori_loop(0, heads, back, 0)
+        run(IN_ATTENTION[s][heads - 1])
 
     run(AFTER_ATTENTION)
-    while small_steps or any(chain[0] for chain in chains.values()):
+    while small_steps or any(chains.values()):
         for name in ("qa", "qb", "qc", "f2a", "f2b", "f2c", "f1a", "f1b", "f1c", "w"):
-            if chains[name][0]:
-                run([name])
+            if chains[name]:
+                do(name)
         if small_steps:
             do("sm")
-    outs.append(fetch(small.at[len(hops)], out_small))
-    input_out(parts - 1)
-    for cp in outs:
-        cp.wait()
+    small_out = fetch(small.at[len(hops)], out_small)
+    ag_in.finish(parts - 1)
+    small_out.wait()
 
 
 def sincos_rows(feature_count):
@@ -828,8 +829,6 @@
         vmem(ff, width),
         vmem32(parts, BLK, width),
         vmem(tokens, width),
-        vmem(tokens, width),
-        vmem(tokens, width),
     ]
     for _ in range(2):
         scratch += [
@@ -839,13 +838,8 @@
         ]
     scratch += [
         vmem32(parts, BLK, width),
-        vmem(heads, HEAD_DIM, tokens),
         vmem32(heads, 1, tokens),
-        vmem32(HEAD_DIM, tokens),
-        vmem(ff, width),
-        vmem(width, ff),
-        vmem(hd, width),
-        vmem(width, 3 * hd),
+        vmem32(heads, tokens, 2 * HEAD_DIM),
         vmem(3 * got(width // 3, 3, log_n), width),
         vmem(3 * got(width // 3, 3, log_n), width),
         vmem(got(hd, 2, log_n), width),
@@ -862,26 +856,25 @@
         pltpu.SemaphoreType.REGULAR((29,)),
         pltpu.SemaphoreType.DMA((4 * parts * 2 + parts + 3 + 10 + 2 + 4 * parts,)),
     ]
-    shape = jax.ShapeDtypeStruct
     hbm = pl.BlockSpec(memory_space=pl.ANY)
     here = pl.BlockSpec(memory_space=pltpu.VMEM)
     results = pl.pallas_call(
         functools.partial(layer_kernel, (parts, log_n, heads)),
         name="layer",
         out_shape=(
-            shape((tokens, width), bf16),
-            shape((tokens, width), bf16),
-            shape((ff, width), bf16),
-            shape((width, ff), bf16),
-            shape((hd, width), bf16),
-            shape((width, 3 * hd), bf16),
-            shape((16, width), f32),
+            vmem(tokens, width),
+            vmem(tokens, width),
+            vmem(ff, width),
+            vmem(width, ff),
+            vmem(hd, width),
+            vmem(width, 3 * hd),
+            jax.ShapeDtypeStruct((16, width), f32),
         ),
         in_specs=[pl.BlockSpec(memory_space=pltpu.SMEM), hbm, hbm, here, here, hbm, hbm, hbm] + [here] * 9,
-        out_specs=(hbm,) * 7,
+        out_specs=(here,) * 6 + (hbm,),
         scratch_shapes=scratch,
         compiler_params=pltpu.CompilerParams(
-            collective_id=0, has_side_effects=True, vmem_limit_bytes=67043328
+            collective_id=0, has_side_effects=True, vmem_limit_bytes=67043328 - 2 * (2 * tokens * width + 2 * ff * width + 4 * hd * width) - 600000
         ),
     )(
         item_lengths,

time: 168 us -> 151 us (0.90)
  Pallas kernels: 152 us -> 138 us
  other arithmetic: 8.3 us -> 6.55 us
    pallas_call x1, Pallas kernels: 152 us -> 138 us  [on_device(): pl.pallas_call(functools.partial(layer_kernel, (parts, log_n, heads)), na...]
    convert_element_type x1, other arithmetic: 4.29 us -> 2.54 us  [on_device(): input_grad.astype(f32)]
where the time goes in v5:
time: 151 us
  Pallas kernels  138 us (91%)
  other arithmetic  6.55 us (4%)
  local copies, waits for them, and re-layouts  5.98 us (4%)
    pallas_call x1, Pallas kernels, on_device(): pl.pallas_call(functools.partial(layer_kernel, (parts, log_n, heads)), na...  138 us

profile of v5, /device:TPU:0, one launch (start us, length us, event | category | flops | bytes accessed | tf_op | source)
XLA Modules:
  0.0 151.2 jit_solution(15154788966877857452)
XLA Ops:
  0.7 138.0 %layer.1 = (bf16[1536,768]{1,0:T(8,128)(2,1)S(1)}, bf16[1536,768]{1,0:T(8,128)(2,1)S(1)}, bf16[768,768]{1,0:T(8,128)(2,1)S(1)}, bf16[768,768]{1,0:T(8,128)(2,1)S...) custom-call(s32[4]{0:T(128)} %lens.1, bf16[1536,768]{1,0:T(8,128)(2,1)} %x_in.1, ...), custom_call_target="tpu_custom_call" | custom-call | tf_op jit(solution)/shard_map/layer/pallas_call | solution.py:861
  138.6 0.0 copy-start
  138.6 1.8 %slice_reduce_fusion = (f32[768]{0:T(1024)}, f32[768]{0:T(1024)}, f32[768]{0:T(1024)}, f32[768]{0:T(1024)}, f32[768]{0:T(1024)}, /*index=5*/f32[768]{0:T(1024)}, f32[768]{0:T(1024)}) fusion(f32[16,768]{1,0:T(8,128)} %get-tuple-element.23), kind=kLoop, calls=%fused_computation | loop fusion | bytes 43008 | tf_op jit(solution)/shard_map/slice | solution.py:913
  140.4 1.3 slice.26
  141.7 2.5 %convert_element_type.13 = f32[1536,768]{1,0:T(8,128)} convert(bf16[1536,768]{1,0:T(8,128)(2,1)S(1)} %get-tuple-element.22) | non-fusion elementwise | flops 1179648 | bytes 7077888 | tf_op jit(solution)/shard_map/convert_element_type | solution.py:901
  144.3 0.0 copy-done
  144.3 1.4 copy.34
  145.7 1.6 %convert_element_type.15 = f32[768,768]{1,0:T(8,128)} convert(bf16[768,768]{1,0:T(8,128)(2,1)S(1)} %get-tuple-element.26) | non-fusion elementwise | flops 589824 | bytes 3538944 | tf_op jit(solution)/shard_map/convert_element_type | solution.py:910
  147.2 0.0 copy-start.1
  147.2 1.6 %convert_element_type.16 = f32[768,768]{1,0:T(8,128)} convert(bf16[768,768]{1,0:T(8,128)(2,1)S(1)} %get-tuple-element.27) | non-fusion elementwise | flops 589824 | bytes 3538944 | tf_op jit(solution)/shard_map/convert_element_type | solution.py:912
  148.8 0.0 copy-done.1
  148.8 1.5 copy.32
  150.3 0.9 convert_element_type.14
Async XLA Ops:
  138.6 5.6 %copy-start = (bf16[768,576]{1,0:T(8,128)(2,1)}, bf16[768,576]{1,0:T(8,128)(2,1)S(1)}, u32[]{:S(2)}) copy-start(bf16[768,576]{1,0:T(8,128)(2,1)S(1)} %get-tuple-element.24) | copy-start | bytes 2654212
  147.2 1.6 %copy-start.1 = (bf16[768,576]{1,0:T(8,128)(2,1)S(1)}, bf16[768,576]{1,0:T(8,128)(2,1)}, u32[]{:S(2)}) copy-start(bf16[768,576]{1,0:T(8,128)(2,1)} %copy-done) | copy-start | bytes 2654212

commit v6 on v5

--- a/solution.py
+++ b/solution.py
@@ -651,11 +651,13 @@
     def small_add(i):
         rows = hops[i][0]
         small_copy(i).wait()
+        if i + 1 == len(hops):
+            out_small[...] = small[i] + small_got[i]
+            return
         small[i + 1, 0:rows] = small[i, 0:rows] + small_got[i, 0:rows]
         if rows < 16:
             small[i + 1, rows:16] = small[i, rows:16]
-        if i + 1 < len(hops):
-            small_copy(i + 1).start()
+        small_copy(i + 1).start()
 
     small_steps = [lambda: small_copy(0).start()] + [
         functools.partial(small_add, i) for i in range(len(hops))
@@ -765,9 +767,7 @@
                 do(name)
         if small_steps:
             do("sm")
-    small_out = fetch(small.at[len(hops)], out_small)
     ag_in.finish(parts - 1)
-    small_out.wait()
 
 
 def sincos_rows(feature_count):
@@ -845,7 +845,7 @@
         vmem(got(hd, 2, log_n), width),
         vmem(3 * got(width // 3, 3, log_n), 3 * hd),
         pltpu.VMEM((tokens, BLK), jnp.int32),
-        vmem32(3 + log_n, 16, width),
+        vmem32(2 + log_n, 16, width),
         vmem32(2 + log_n, 16, width),
         vmem32(8, ff),
     ]
@@ -868,13 +868,13 @@
             vmem(width, ff),
             vmem(hd, width),
             vmem(width, 3 * hd),
-            jax.ShapeDtypeStruct((16, width), f32),
+            vmem32(16, width),
         ),
         in_specs=[pl.BlockSpec(memory_space=pltpu.SMEM), hbm, hbm, here, here, hbm, hbm, hbm] + [here] * 9,
-        out_specs=(here,) * 6 + (hbm,),
+        out_specs=(here,) * 7,
         scratch_shapes=scratch,
         compiler_params=pltpu.CompilerParams(
-            collective_id=0, has_side_effects=True, vmem_limit_bytes=67043328 - 2 * (2 * tokens * width + 2 * ff * width + 4 * hd * width) - 600000
+            collective_id=0, has_side_effects=True, vmem_limit_bytes=67043328 - 2 * (2 * tokens * width + 2 * ff * width + 4 * hd * width) - 64 * width - 600000
         ),
     )(
         item_lengths,

time: 151 us -> 149 us (0.987)
  local copies, waits for them, and re-layouts: 5.98 us -> 4.23 us
where the time goes in v6:
time: 149 us
  Pallas kernels  137 us (92%)
  other arithmetic  6.55 us (4%)
  local copies, waits for them, and re-layouts  4.23 us (3%)
    pallas_call x1, Pallas kernels, on_device(): pl.pallas_call(functools.partial(layer_kernel, (parts, log_n, heads)), na...  137 us

profile of v6, /device:TPU:0, one launch (start us, length us, event | category | flops | bytes accessed | tf_op | source)
XLA Modules:
  0.0 148.9 jit_solution(12975658045570333480)
XLA Ops:
  0.7 137.4 %layer.1 = (bf16[1536,768]{1,0:T(8,128)(2,1)S(1)}, bf16[1536,768]{1,0:T(8,128)(2,1)S(1)}, bf16[768,768]{1,0:T(8,128)(2,1)S(1)}, bf16[768,768]{1,0:T(8,128)(2,1)S...) custom-call(s32[4]{0:T(128)} %lens.1, bf16[1536,768]{1,0:T(8,128)(2,1)} %x_in.1, ...), custom_call_target="tpu_custom_call" | custom-call | tf_op jit(solution)/shard_map/layer/pallas_call | solution.py:861
  138.1 0.0 copy-start
  138.1 0.7 slice_reduce_fusion
  138.8 0.6 slice.26
  139.4 2.5 %convert_element_type.13 = f32[1536,768]{1,0:T(8,128)} convert(bf16[1536,768]{1,0:T(8,128)(2,1)S(1)} %get-tuple-element.22) | non-fusion elementwise | flops 1179648 | bytes 7077888 | tf_op jit(solution)/shard_map/convert_element_type | solution.py:901
  142.0 0.0 copy-done
  142.0 1.4 copy.34
  143.4 1.6 %convert_element_type.15 = f32[768,768]{1,0:T(8,128)} convert(bf16[768,768]{1,0:T(8,128)(2,1)S(1)} %get-tuple-element.26) | non-fusion elementwise | flops 589824 | bytes 3538944 | tf_op jit(solution)/shard_map/convert_element_type | solution.py:910
  144.9 0.0 copy-start.1
  144.9 1.6 %convert_element_type.16 = f32[768,768]{1,0:T(8,128)} convert(bf16[768,768]{1,0:T(8,128)(2,1)S(1)} %get-tuple-element.27) | non-fusion elementwise | flops 589824 | bytes 3538944 | tf_op jit(solution)/shard_map/convert_element_type | solution.py:912
  146.5 0.0 copy-done.1
  146.5 1.5 %copy.32 = f32[768,576]{0,1:T(8,128)} copy(bf16[768,576]{1,0:T(8,128)(2,1)S(1)} %copy-done.1) | data formatting | bytes 2654208 | tf_op jit(solution)/shard_map/reshape | solution.py:904
  148.0 0.9 convert_element_type.14
Async XLA Ops:
  138.1 3.9 %copy-start = (bf16[768,576]{1,0:T(8,128)(2,1)}, bf16[768,576]{1,0:T(8,128)(2,1)S(1)}, u32[]{:S(2)}) copy-start(bf16[768,576]{1,0:T(8,128)(2,1)S(1)} %get-tuple-element.24) | copy-start | bytes 2654212
  144.9 1.6 %copy-start.1 = (bf16[768,576]{1,0:T(8,128)(2,1)S(1)}, bf16[768,576]{1,0:T(8,128)(2,1)}, u32[]{:S(2)}) copy-start(bf16[768,576]{1,0:T(8,128)(2,1)} %copy-done) | copy-start | bytes 2654212
